TPU v7x, 32 devices: a whole 2x2x4 slice. The times are simulated.
32 devices in a mesh: row: 4 (over y, x), col: 8 (over z, core).
Axes of the slice: x: 2, y: 2, z: 4, core: 2. Of those that a mesh axis runs over, the one named last changes fastest.
Arguments:
- features: bfloat16 [8192, 512], P(('col', 'row')), may hold values from -6 to 6
- order: int32 [8192], P('col'), may hold values from 0 to 8191, as said below
- tile_count: int32 [4, 8], P('row', 'col'), may hold values from 1 to 16, as said below
- tile_slots: int32 [4, 8, 16], P('row', 'col'), may hold values from 0 to 127, as said below
- blocks: bfloat16 [4, 8, 16, 128, 128], P('row', 'col'), may hold values from -0.3125 to 0.3125
- weight: bfloat16 [512, 512], replicated, may hold values from -0.25 to 0.25
Outputs:
- updated: bfloat16 [8192, 512], P(('row', 'col'))
Inputs may be any that keep to these rules, and one draw needn't show every extreme that they name: order permutes each column group: positions j * 8 * 128 to (j + 1) * 8 * 128 - 1 name each node of that same range once. `tile_count`: some tile lists exactly 16 blocks in every draw. `tile_slots`: the codes of one tile's slots are distinct; slots at or beyond its count are unused.
All inputs are finite; a program needn't handle non-finite values.
Results may differ from a plain program's by a relative error of at most 0.01.
Values may be sent and summed in bfloat16 or wider, within the bound.
No kernel may reach another device: no remote copies, remote signals or barrier semaphores. Data moves between devices by JAX's collectives and lax.ppermute only.
A program may use at most 64 MiB of HBM per device.

v0:
```python
import functools

import jax
import jax.numpy as jnp
from jax import lax
from jax.experimental import pallas as pl
from jax.experimental.pallas import tpu as pltpu
from jax.sharding import PartitionSpec as P

VMEM_LIMIT = 16 * 1024 * 1024
SHARES = (1, 1)
COST = 10**10


def cut_kernel(x_hbm, *refs):
    outs, sems = refs[:-1], refs[-1]
    copies, start = [], 0
    for k, out in enumerate(outs):
        depth = out.shape[1]
        copies.append(pltpu.make_async_copy(x_hbm.at[:, pl.ds(start, depth)], out, sems.at[k]))
        start += depth
    for copy in copies:
        copy.start()
    for copy in copies:
        copy.wait()


def place_of(slot, core, bits):
    near = 0
    for bit in range(bits):
        near += ((slot >> (bit + 1)) & 1) << (bits - 1 - bit)
    return jnp.where(core == 0, near, slot >> 1)


def tile_kernel(bits, rows, shard, order_hbm, blocks_hbm, count_ref, slots_ref, give_ref, keep_ref, pick_ref,
                order_ref, blocks_ref, sems):
    copies = [
        pltpu.make_async_copy(src, dst, sems.at[k])
        for k, (src, dst) in enumerate(((order_hbm, order_ref), (blocks_hbm, blocks_ref)))
    ]
    for copy in copies:
        copy.start()
    group = keep_ref.shape[1]
    width = blocks_ref.shape[-1]
    colblk = group // width
    piece = min(rows, width)
    me = lax.axis_index("col")
    row = lax.axis_index("row")
    keep_ref[...] = jnp.zeros_like(keep_ref)
    give_ref[...] = jnp.zeros_like(give_ref)
    place = lax.broadcasted_iota(jnp.int32, (width, group), 1)
    corpus = ((place // shard) ^ row) * shard + place % shard + me * group
    copies[0].wait()
    nodes = jnp.broadcast_to(order_ref[...][:, None, :], (colblk, width // colblk, width))
    nodes = nodes.reshape(width, width).T
    for k in range(colblk):
        column = nodes[:, k * (width // colblk):k * (width // colblk) + 1]
        pick_ref[k * width:(k + 1) * width, :] = jnp.where(corpus == column, 1.0, 0.0).astype(pick_ref.dtype)
    copies[1].wait()

    def step(index, carry):
        code = slots_ref[0, 0, index]
        columns = pl.ds(pl.multiple_of(lax.rem(code, colblk) * width, width), width)
        for part in range(width // piece):
            start = code // colblk * width + part * piece
            slot = (start // rows) ^ me
            at = place_of(slot, (me ^ slot) & 1, bits) * rows + lax.rem(start, rows)
            at = pl.ds(pl.multiple_of(at, piece), piece)
            values = blocks_ref[0, 0, index, part * piece:(part + 1) * piece, :]

            @pl.when(slot & 1 == 0)
            def _():
                keep_ref[at, columns] = values

            @pl.when(slot & 1 == 1)
            def _():
                give_ref[at, columns] = values

        return carry

    lax.fori_loop(0, count_ref[0, 0], step, 0)


def order_kernel(pick_ref, *refs):
    features, ordered_ref = refs[:-1], refs[-1]
    x = jnp.concatenate([ref[...] for ref in features], axis=0)
    ordered_ref[...] = jnp.dot(pick_ref[...], x, preferred_element_type=jnp.float32).astype(ordered_ref.dtype)


def sum_kernel(tile_ref, ordered_ref, out_ref):
    out_ref[...] = jnp.dot(tile_ref[...], ordered_ref[...], preferred_element_type=jnp.float32).astype(out_ref.dtype)


def add_kernel(mine_ref, got_ref, hold_ref, *sends):
    count = hold_ref.shape[0]
    hold_ref[...] = mine_ref[:count, :] + got_ref[:count, :].astype(jnp.float32)
    for send_ref in sends:
        here = slice(count, count + send_ref.shape[0])
        send_ref[...] = (mine_ref[here, :] + got_ref[here, :].astype(jnp.float32)).astype(send_ref.dtype)
        count += send_ref.shape[0]


def relay_kernel(mine_ref, got_ref, *sends):
    offset = got_ref.shape[0]
    start = 0
    for send_ref in sends:
        count = send_ref.shape[0]
        total = mine_ref[offset + start:offset + start + count, :] + got_ref[start:start + count, :].astype(jnp.float32)
        send_ref[...] = total.astype(send_ref.dtype)
        start += count


def keep_kernel(mine_ref, got_ref, hold_ref):
    hold_ref[...] = mine_ref[:hold_ref.shape[0], :] + got_ref[...].astype(jnp.float32)


def project_kernel(*refs):
    weight_ref, out_ref = refs[-2], refs[-1]
    projected, start = None, 0
    for part in range((len(refs) - 2) // 3):
        mine_ref, near_ref, far_ref = refs[3 * part:3 * part + 3]
        total = mine_ref[:near_ref.shape[0], :] + near_ref[...].astype(jnp.float32) + far_ref[...].astype(jnp.float32)
        depth = total.shape[1]
        product = jnp.dot(
            total.astype(jnp.bfloat16), weight_ref[start:start + depth, :], preferred_element_type=jnp.float32
        )
        projected = product if projected is None else projected + product
        start += depth
    out_ref[...] = jnp.maximum(projected, 0.0).astype(out_ref.dtype)


def per_device(features, order, tile_count, tile_slots, blocks, weight):
    rows_axis, cols_axis = lax.axis_size("row"), lax.axis_size("col")
    bits = cols_axis.bit_length() - 2
    half = cols_axis // 2
    shard, feats = features.shape
    group = shard * rows_axis
    width = blocks.shape[-1]
    rows = shard
    params = pltpu.CompilerParams(vmem_limit_bytes=VMEM_LIMIT)
    vmem = pl.BlockSpec(memory_space=pltpu.VMEM)
    smem = pl.BlockSpec(memory_space=pltpu.SMEM)
    hbm = pl.BlockSpec(memory_space=pltpu.HBM)
    bf16, f32 = jnp.bfloat16, jnp.float32
    shape = jax.ShapeDtypeStruct

    def call(kernel, outs, ins, specs=None, scratch=(), cost=COST):
        return pl.pallas_call(
            kernel,
            out_shape=outs,
            in_specs=specs or [vmem] * len(ins),
            out_specs=jax.tree.map(lambda _: vmem, outs),
            scratch_shapes=scratch,
            compiler_params=params,
            cost_estimate=pl.CostEstimate(flops=cost, bytes_accessed=cost, transcendentals=0),
        )(*ins)

    def in_hbm(x):
        return pltpu.with_memory_space_constraint(x, pltpu.HBM)

    def after(x, *done):
        return lax.optimization_barrier((x, *done))[0]

    def exchange(x, axis, distance):
        return lax.ppermute(x, axis, [(i, i ^ distance) for i in range(lax.axis_size(axis))])

    def exchange_chips(x, step):
        far = cols_axis >> (step + 1)
        near = 2 << step
        return lax.ppermute(x, "col", [(j, j ^ (far if j & 1 else near)) for j in range(cols_axis)])

    widths = [feats * share // sum(SHARES) for share in SHARES]
    cuts = call(
        cut_kernel, [shape((shard, depth), bf16) for depth in widths], [in_hbm(features)],
        [hbm], [pltpu.SemaphoreType.DMA((len(widths),))], 1,
    )
    gathered = [[mine] + [exchange(mine, "row", k) for k in range(1, rows_axis)] for mine in cuts]
    table = (group // width, width)
    give, keep, pick = call(
        functools.partial(tile_kernel, bits, rows, shard),
        [shape((half * rows, group), bf16)] * 2 + [shape((group, group), bf16)],
        [in_hbm(order.reshape(table)), in_hbm(blocks), tile_count, tile_slots],
        [hbm, hbm, smem, smem],
        [
            pltpu.VMEM(table, jnp.int32),
            pltpu.VMEM(blocks.shape, bf16),
            pltpu.SemaphoreType.DMA((2,)),
        ],
    )

    def pieces(count, depth):
        return [shape((count // 2 * rows, depth), bf16)] * 2 if count > 1 else [shape((rows, depth), bf16)]

    def first_step(mine, got):
        depth = mine.shape[1]
        outs = [shape((half // 2 * rows, depth), f32)] + pieces(half // 2, depth)
        hold, low, high = call(add_kernel, outs, [mine, got])
        return hold, exchange_chips(high, 0), exchange_chips(low, 0)

    def later_steps(hold, high, low):
        step, depth = 1, hold.shape[1]
        while True:
            count = hold.shape[0] // (2 * rows)
            sends = call(relay_kernel, pieces(count, depth), [hold, high])
            sent[:] = sends
            if count == 1:
                return [hold, low, exchange_chips(sends[0], step)]
            hold = call(keep_kernel, shape((count * rows, depth), f32), [hold, low])
            low, high = [exchange_chips(send, step) for send in sends]
            step += 1

    ends, waiting, sent, lows = [], None, [], []
    for features, depth in zip(gathered, widths, strict=True):
        if waiting is not None:
            features = [after(features[0], waiting[0]), *features[1:]]
        ordered = call(order_kernel, shape((group, depth), bf16), [pick, *features])
        given = call(sum_kernel, shape((half * rows, depth), bf16), [give, ordered])
        got = exchange(given, "col", 1)
        if waiting is not None:
            ends += later_steps(waiting[0], after(waiting[1], given), waiting[2])
            ordered = after(ordered, sent[0])
        mine = call(sum_kernel, shape((half * rows, depth), f32), [keep, ordered])
        waiting = first_step(mine, got)
        lows.append(waiting[2])
    ends += later_steps(waiting[0], after(waiting[1], *lows[:-1], *ends[2::3]), waiting[2])
    return call(project_kernel, shape((rows, feats), bf16), [*ends, weight])


def solution(mesh):
    in_specs = (
        P(("col", "row"), None),
        P("col"),
        P("row", "col"),
        P("row", "col", None),
        P("row", "col", None, None, None),
        P(),
    )
    out_specs = P(("row", "col"), None)
    return jax.shard_map(
        per_device, mesh=mesh, in_specs=in_specs, out_specs=out_specs, check_vma=False
    )
```

profile of v0, /device:TPU:30, one launch (start us, length us, event | category | flops | bytes accessed | tf_op | source)
XLA Modules:
  0.0 40.3 jit_solution(15946145559955445231)
XLA Ops:
  0.0 1.0 %shard_map.65 = (bf16[256,256]{1,0:T(8,128)(2,1)S(1)}, bf16[256,256]{1,0:T(8,128)(2,1)S(1)}) custom-call(bf16[256,512]{1,0:T(8,128)(2,1)} %x_hbm.1), custom_call_target="tpu_custom_call" | custom-call | flops 1 | bytes 1 | tf_op jit(solution)/shard_map/pallas_call | solution.py:148
  1.0 0.6 %collective-permute-start = (bf16[256,256]{1,0:T(8,128)(2,1)S(1)}, bf16[256,256]{1,0:T(8,128)(2,1)S(1)}, u32[]{:S(2)}, u32[]{:S(2)}) collective-permute-start(bf16[256,256]{1,0:T(8,128)(2,1)S(1)} %get-tuple-element.22.refs_0_), channel_id=1, source_target_pairs={{0,8},{8,0},{16,24},{24,16},{1,9},{9,1},{17,25},{25,17},{2,10},{10... | collective-permute-start | bytes 393224 | tf_op jit(solution)/shard_map/ppermute | solution.py:165
  1.6 0.5 %collective-permute-start.1 = (bf16[256,256]{1,0:T(8,128)(2,1)S(1)}, bf16[256,256]{1,0:T(8,128)(2,1)S(1)}, u32[]{:S(2)}, u32[]{:S(2)}) collective-permute-start(bf16[256,256]{1,0:T(8,128)(2,1)S(1)} %get-tuple-element.22.refs_0_), channel_id=1, source_target_pairs={{0,16},{8,24},{16,0},{24,8},{1,17},{9,25},{17,1},{25,9},{2,18},{10... | collective-permute-start | bytes 393224 | tf_op jit(solution)/shard_map/ppermute | solution.py:165
  2.1 2.4 %collective-permute-start.2 = (bf16[256,256]{1,0:T(8,128)(2,1)S(1)}, bf16[256,256]{1,0:T(8,128)(2,1)S(1)}, u32[]{:S(2)}, u32[]{:S(2)}) collective-permute-start(bf16[256,256]{1,0:T(8,128)(2,1)S(1)} %get-tuple-element.22.refs_0_), channel_id=1, source_target_pairs={{0,24},{8,16},{16,8},{24,0},{1,25},{9,17},{17,9},{25,1},{2,26},{10... | collective-permute-start | bytes 393224 | tf_op jit(solution)/shard_map/ppermute | solution.py:165
  4.5 0.5 %collective-permute-start.6 = (bf16[256,256]{1,0:T(8,128)(2,1)S(1)}, bf16[256,256]{1,0:T(8,128)(2,1)S(1)}, u32[]{:S(2)}, u32[]{:S(2)}) collective-permute-start(bf16[256,256]{1,0:T(8,128)(2,1)S(1)} %get-tuple-element.28.refs_0_), channel_id=1, source_target_pairs={{0,8},{8,0},{16,24},{24,16},{1,9},{9,1},{17,25},{25,17},{2,10},{10... | collective-permute-start | bytes 393224 | tf_op jit(solution)/shard_map/ppermute | solution.py:165
  5.1 0.5 %collective-permute-start.7 = (bf16[256,256]{1,0:T(8,128)(2,1)S(1)}, bf16[256,256]{1,0:T(8,128)(2,1)S(1)}, u32[]{:S(2)}, u32[]{:S(2)}) collective-permute-start(bf16[256,256]{1,0:T(8,128)(2,1)S(1)} %get-tuple-element.28.refs_0_), channel_id=1, source_target_pairs={{0,16},{8,24},{16,0},{24,8},{1,17},{9,25},{17,1},{25,9},{2,18},{10... | collective-permute-start | bytes 393224 | tf_op jit(solution)/shard_map/ppermute | solution.py:165
  6.3 0.6 %copy-done.1 = s32[1,1,16]{2,1,0:T(1,128)S(1)} copy-done((s32[1,1,16]{2,1,0:T(1,128)S(1)}, s32[1,1,16]{2,1,0:T(1,128)}, u32[]{:S(2)}) %copy-start.1) | copy-done | bytes 88
  6.9 2.0 %shard_map.64 = (bf16[1024,1024]{1,0:T(8,128)(2,1)S(1)}, bf16[1024,1024]{1,0:T(8,128)(2,1)S(1)}, bf16[1024,1024]{1,0:T(8,128)(2,1)S(1)}) custom-call(s32[8,128]{1,0:T(8,128)} %bitcast.1, bf16[1,1,16,128,128]{4,3,2,1,0:T(8,128)(2,1)} %blocks_hbm.1, s32[1,1]{1,0:T(1,128)S(6)} %copy.7.count_ref, s32[1,1,16]{2,1,0:T(1,128)S(1)} %copy-done.1), custom_call_target="tpu_custom_call" | custom-call | flops 10000000000 | bytes 10000000000 | tf_op jit(solution)/shard_map/pallas_call | solution.py:148
  8.9 2.8 %collective-permute-start.8 = (bf16[256,256]{1,0:T(8,128)(2,1)S(1)}, bf16[256,256]{1,0:T(8,128)(2,1)S(1)}, u32[]{:S(2)}, u32[]{:S(2)}) collective-permute-start(bf16[256,256]{1,0:T(8,128)(2,1)S(1)} %get-tuple-element.28.refs_0_), channel_id=1, source_target_pairs={{0,24},{8,16},{16,8},{24,0},{1,25},{9,17},{17,9},{25,1},{2,26},{10... | collective-permute-start | bytes 393224 | tf_op jit(solution)/shard_map/ppermute | solution.py:165
  11.7 0.7 %shard_map.66.ordered_ref = bf16[1024,256]{1,0:T(8,128)(2,1)S(1)} custom-call(bf16[1024,1024]{1,0:T(8,128)(2,1)S(1)} %get-tuple-element.21.pick_ref, bf16[256,256]{1,0:T(8,128)(2,1)S(1)} %get-tuple-element.22.refs_0_, bf16[256,256]{1,0:T(8,128)(2,1)S(1)} %collective-permute-done.refs_1_, bf16[256,256]{1,0:T(8,128)(2,1)S(1)} %collective-permute-done.1.refs_2_, ...), custom_call_target="tpu_custom_call" | custom-call | flops 10000000000 | bytes 10000000000 | tf_op jit(solution)/shard_map/pallas_call | solution.py:148
  12.4 0.7 %shard_map.68 = bf16[1024,256]{1,0:T(8,128)(2,1)S(1)} custom-call(bf16[1024,1024]{1,0:T(8,128)(2,1)S(1)} %get-tuple-element.23.tile_ref, bf16[1024,256]{1,0:T(8,128)(2,1)S(1)} %shard_map.66.ordered_ref), custom_call_target="tpu_custom_call" | custom-call | flops 10000000000 | bytes 10000000000 | tf_op jit(solution)/shard_map/pallas_call | solution.py:148
  13.2 0.7 %shard_map.67.mine_ref = f32[1024,256]{1,0:T(8,128)S(1)} custom-call(bf16[1024,1024]{1,0:T(8,128)(2,1)S(1)} %get-tuple-element.20.tile_ref, bf16[1024,256]{1,0:T(8,128)(2,1)S(1)} %shard_map.66.ordered_ref), custom_call_target="tpu_custom_call" | custom-call | flops 10000000000 | bytes 10000000000 | tf_op jit(solution)/shard_map/pallas_call | solution.py:148
  13.9 1.2 %collective-permute-done.3.got_ref = bf16[1024,256]{1,0:T(8,128)(2,1)S(1)} collective-permute-done((bf16[1024,256]{1,0:T(8,128)(2,1)S(1)}, bf16[1024,256]{1,0:T(8,128)(2,1)S(1)}, u32[]{:S(2)}, u32[]{:S(2)}) %collective-permute-start.3) | collective-permute-done | bytes 524320 | tf_op jit(solution)/shard_map/ppermute | solution.py:165
  15.2 0.3 collective-permute-start.5
  15.5 0.7 %shard_map.70.ordered_ref = bf16[1024,256]{1,0:T(8,128)(2,1)S(1)} custom-call(bf16[1024,1024]{1,0:T(8,128)(2,1)S(1)} %get-tuple-element.21.pick_ref, bf16[256,256]{1,0:T(8,128)(2,1)S(1)} %get-tuple-element.28.refs_0_, bf16[256,256]{1,0:T(8,128)(2,1)S(1)} %collective-permute-done.6.refs_1_, bf16[256,256]{1,0:T(8,128)(2,1)S(1)} %collective-permute-done.7.refs_2_, ...), custom_call_target="tpu_custom_call" | custom-call | flops 10000000000 | bytes 10000000000 | tf_op jit(solution)/shard_map/pallas_call | solution.py:148
  16.2 0.7 %shard_map.71 = bf16[1024,256]{1,0:T(8,128)(2,1)S(1)} custom-call(bf16[1024,1024]{1,0:T(8,128)(2,1)S(1)} %get-tuple-element.23.tile_ref, bf16[1024,256]{1,0:T(8,128)(2,1)S(1)} %shard_map.70.ordered_ref), custom_call_target="tpu_custom_call" | custom-call | flops 10000000000 | bytes 10000000000 | tf_op jit(solution)/shard_map/pallas_call | solution.py:148
  17.0 1.9 %collective-permute-start.4 = (bf16[256,256]{1,0:T(8,128)(2,1)S(1)}, bf16[256,256]{1,0:T(8,128)(2,1)S(1)}, u32[]{:S(2)}, u32[]{:S(2)}) collective-permute-start(bf16[256,256]{1,0:T(8,128)(2,1)S(1)} %get-tuple-element.25), channel_id=1, source_target_pairs={{0,2},{1,5},{2,0},{3,7},{4,6},{5,1},{6,4},{7,3},{8,10},{9,13},{10,... | collective-permute-start | bytes 393224 | tf_op jit(solution)/shard_map/ppermute | solution.py:170
  18.9 3.6 %collective-permute-done.5.got_ref = bf16[256,256]{1,0:T(8,128)(2,1)S(1)} collective-permute-done((bf16[256,256]{1,0:T(8,128)(2,1)S(1)}, bf16[256,256]{1,0:T(8,128)(2,1)S(1)}, u32[]{:S(2)}, u32[]{:S(2)}) %collective-permute-start.5) | collective-permute-done | bytes 131104 | tf_op jit(solution)/shard_map/ppermute | solution.py:170
  22.6 0.7 %shard_map.73.mine_ref = f32[1024,256]{1,0:T(8,128)S(1)} custom-call(bf16[1024,1024]{1,0:T(8,128)(2,1)S(1)} %get-tuple-element.20.tile_ref, bf16[1024,256]{1,0:T(8,128)(2,1)S(1)} %shard_map.70.ordered_ref), custom_call_target="tpu_custom_call" | custom-call | flops 10000000000 | bytes 10000000000 | tf_op jit(solution)/shard_map/pallas_call | solution.py:148
  23.3 0.1 shard_map.74
  23.5 2.0 %collective-permute-start.11 = (bf16[256,256]{1,0:T(8,128)(2,1)S(1)}, bf16[256,256]{1,0:T(8,128)(2,1)S(1)}, u32[]{:S(2)}, u32[]{:S(2)}) collective-permute-start(bf16[256,256]{1,0:T(8,128)(2,1)S(1)} %get-tuple-element.32), channel_id=1, source_target_pairs={{0,2},{1,5},{2,0},{3,7},{4,6},{5,1},{6,4},{7,3},{8,10},{9,13},{10,... | collective-permute-start | bytes 393224 | tf_op jit(solution)/shard_map/ppermute | solution.py:170
  25.5 7.7 %collective-permute-done.9.refs_2_ = bf16[256,256]{1,0:T(8,128)(2,1)S(1)} collective-permute-done((bf16[256,256]{1,0:T(8,128)(2,1)S(1)}, bf16[256,256]{1,0:T(8,128)(2,1)S(1)}, u32[]{:S(2)}, u32[]{:S(2)}) %collective-permute-start.9) | collective-permute-done | bytes 131104 | tf_op jit(solution)/shard_map/ppermute | solution.py:170
  33.4 5.8 %collective-permute-done.13.refs_5_ = bf16[256,256]{1,0:T(8,128)(2,1)S(1)} collective-permute-done((bf16[256,256]{1,0:T(8,128)(2,1)S(1)}, bf16[256,256]{1,0:T(8,128)(2,1)S(1)}, u32[]{:S(2)}, u32[]{:S(2)}) %collective-permute-start.13) | collective-permute-done | bytes 131104 | tf_op jit(solution)/shard_map/ppermute | solution.py:170
  39.2 1.0 %shard_map.76 = bf16[256,512]{1,0:T(8,128)(2,1)} custom-call(f32[512,256]{1,0:T(8,128)S(1)} %get-tuple-element.24.mine_ref.refs_0_, bf16[256,256]{1,0:T(8,128)(2,1)S(1)} %collective-permute-done.4.refs_1_, bf16[256,256]{1,0:T(8,128)(2,1)S(1)} %collective-permute-done.9.refs_2_, f32[512,256]{1,0:T(8,128)S(1)} %get-tuple-element.31.mine_ref.refs_3_, ...), custom_call_target="tpu_custom_call" | custom-call | flops 10000000000 | bytes 10000000000 | tf_op jit(solution)/shard_map/pallas_call | solution.py:148
  (21 shorter events, 0.5 us)
Async XLA Ops:
  1.0 7.9 %collective-permute-start = (bf16[256,256]{1,0:T(8,128)(2,1)S(1)}, bf16[256,256]{1,0:T(8,128)(2,1)S(1)}, u32[]{:S(2)}, u32[]{:S(2)}) collective-permute-start(bf16[256,256]{1,0:T(8,128)(2,1)S(1)} %get-tuple-element.22.refs_0_), channel_id=1, source_target_pairs={{0,8},{8,0},{16,24},{24,16},{1,9},{9,1},{17,25},{25,17},{2,10},{10... | collective-permute-start | bytes 393224 | tf_op jit(solution)/shard_map/ppermute | solution.py:165
  1.6 10.1 %collective-permute-start.1 = (bf16[256,256]{1,0:T(8,128)(2,1)S(1)}, bf16[256,256]{1,0:T(8,128)(2,1)S(1)}, u32[]{:S(2)}, u32[]{:S(2)}) collective-permute-start(bf16[256,256]{1,0:T(8,128)(2,1)S(1)} %get-tuple-element.22.refs_0_), channel_id=1, source_target_pairs={{0,16},{8,24},{16,0},{24,8},{1,17},{9,25},{17,1},{25,9},{2,18},{10... | collective-permute-start | bytes 393224 | tf_op jit(solution)/shard_map/ppermute | solution.py:165
  2.1 9.6 %collective-permute-start.2 = (bf16[256,256]{1,0:T(8,128)(2,1)S(1)}, bf16[256,256]{1,0:T(8,128)(2,1)S(1)}, u32[]{:S(2)}, u32[]{:S(2)}) collective-permute-start(bf16[256,256]{1,0:T(8,128)(2,1)S(1)} %get-tuple-element.22.refs_0_), channel_id=1, source_target_pairs={{0,24},{8,16},{16,8},{24,0},{1,25},{9,17},{17,9},{25,1},{2,26},{10... | collective-permute-start | bytes 393224 | tf_op jit(solution)/shard_map/ppermute | solution.py:165
  4.5 10.9 %collective-permute-start.6 = (bf16[256,256]{1,0:T(8,128)(2,1)S(1)}, bf16[256,256]{1,0:T(8,128)(2,1)S(1)}, u32[]{:S(2)}, u32[]{:S(2)}) collective-permute-start(bf16[256,256]{1,0:T(8,128)(2,1)S(1)} %get-tuple-element.28.refs_0_), channel_id=1, source_target_pairs={{0,8},{8,0},{16,24},{24,16},{1,9},{9,1},{17,25},{25,17},{2,10},{10... | collective-permute-start | bytes 393224 | tf_op jit(solution)/shard_map/ppermute | solution.py:165
  5.1 10.4 %collective-permute-start.7 = (bf16[256,256]{1,0:T(8,128)(2,1)S(1)}, bf16[256,256]{1,0:T(8,128)(2,1)S(1)}, u32[]{:S(2)}, u32[]{:S(2)}) collective-permute-start(bf16[256,256]{1,0:T(8,128)(2,1)S(1)} %get-tuple-element.28.refs_0_), channel_id=1, source_target_pairs={{0,16},{8,24},{16,0},{24,8},{1,17},{9,25},{17,1},{25,9},{2,18},{10... | collective-permute-start | bytes 393224 | tf_op jit(solution)/shard_map/ppermute | solution.py:165
  6.2 0.7 %copy-start.1 = (s32[1,1,16]{2,1,0:T(1,128)S(1)}, s32[1,1,16]{2,1,0:T(1,128)}, u32[]{:S(2)}) copy-start(s32[1,1,16]{2,1,0:T(1,128)} %slots_ref.1) | copy-start | bytes 196
  8.9 6.6 %collective-permute-start.8 = (bf16[256,256]{1,0:T(8,128)(2,1)S(1)}, bf16[256,256]{1,0:T(8,128)(2,1)S(1)}, u32[]{:S(2)}, u32[]{:S(2)}) collective-permute-start(bf16[256,256]{1,0:T(8,128)(2,1)S(1)} %get-tuple-element.28.refs_0_), channel_id=1, source_target_pairs={{0,24},{8,16},{16,8},{24,0},{1,25},{9,17},{17,9},{25,1},{2,26},{10... | collective-permute-start | bytes 393224 | tf_op jit(solution)/shard_map/ppermute | solution.py:165
  13.1 2.0 %collective-permute-start.3 = (bf16[1024,256]{1,0:T(8,128)(2,1)S(1)}, bf16[1024,256]{1,0:T(8,128)(2,1)S(1)}, u32[]{:S(2)}, u32[]{:S(2)}) collective-permute-start(bf16[1024,256]{1,0:T(8,128)(2,1)S(1)} %shard_map.68), channel_id=1, source_target_pairs={{0,1},{1,0},{2,3},{3,2},{4,5},{5,4},{6,7},{7,6},{8,9},{9,8},{10,11... | collective-permute-start | bytes 1572872 | tf_op jit(solution)/shard_map/ppermute | solution.py:165
  15.2 7.3 %collective-permute-start.5 = (bf16[256,256]{1,0:T(8,128)(2,1)S(1)}, bf16[256,256]{1,0:T(8,128)(2,1)S(1)}, u32[]{:S(2)}, u32[]{:S(2)}) collective-permute-start(bf16[256,256]{1,0:T(8,128)(2,1)S(1)} %get-tuple-element.26), channel_id=1, source_target_pairs={{0,2},{1,5},{2,0},{3,7},{4,6},{5,1},{6,4},{7,3},{8,10},{9,13},{10,... | collective-permute-start | bytes 393224 | tf_op jit(solution)/shard_map/ppermute | solution.py:170
  16.9 6.4 %collective-permute-start.10 = (bf16[1024,256]{1,0:T(8,128)(2,1)S(1)}, bf16[1024,256]{1,0:T(8,128)(2,1)S(1)}, u32[]{:S(2)}, u32[]{:S(2)}) collective-permute-start(bf16[1024,256]{1,0:T(8,128)(2,1)S(1)} %shard_map.71), channel_id=1, source_target_pairs={{0,1},{1,0},{2,3},{3,2},{4,5},{5,4},{6,7},{7,6},{8,9},{9,8},{10,11... | collective-permute-start | bytes 1572872 | tf_op jit(solution)/shard_map/ppermute | solution.py:165
  17.0 8.6 %collective-permute-start.4 = (bf16[256,256]{1,0:T(8,128)(2,1)S(1)}, bf16[256,256]{1,0:T(8,128)(2,1)S(1)}, u32[]{:S(2)}, u32[]{:S(2)}) collective-permute-start(bf16[256,256]{1,0:T(8,128)(2,1)S(1)} %get-tuple-element.25), channel_id=1, source_target_pairs={{0,2},{1,5},{2,0},{3,7},{4,6},{5,1},{6,4},{7,3},{8,10},{9,13},{10,... | collective-permute-start | bytes 393224 | tf_op jit(solution)/shard_map/ppermute | solution.py:170
  22.5 10.7 %collective-permute-start.9 = (bf16[256,256]{1,0:T(8,128)(2,1)S(1)}, bf16[256,256]{1,0:T(8,128)(2,1)S(1)}, u32[]{:S(2)}, u32[]{:S(2)}) collective-permute-start(bf16[256,256]{1,0:T(8,128)(2,1)S(1)} %shard_map.72), channel_id=1, source_target_pairs={{0,4},{1,3},{2,6},{3,1},{4,0},{5,7},{6,2},{7,5},{8,12},{9,11},{10,... | collective-permute-start | bytes 393224 | tf_op jit(solution)/shard_map/ppermute | solution.py:170
  23.4 9.8 %collective-permute-start.12 = (bf16[256,256]{1,0:T(8,128)(2,1)S(1)}, bf16[256,256]{1,0:T(8,128)(2,1)S(1)}, u32[]{:S(2)}, u32[]{:S(2)}) collective-permute-start(bf16[256,256]{1,0:T(8,128)(2,1)S(1)} %get-tuple-element.33), channel_id=1, source_target_pairs={{0,2},{1,5},{2,0},{3,7},{4,6},{5,1},{6,4},{7,3},{8,10},{9,13},{10,... | collective-permute-start | bytes 393224 | tf_op jit(solution)/shard_map/ppermute | solution.py:170
  23.5 9.9 %collective-permute-start.11 = (bf16[256,256]{1,0:T(8,128)(2,1)S(1)}, bf16[256,256]{1,0:T(8,128)(2,1)S(1)}, u32[]{:S(2)}, u32[]{:S(2)}) collective-permute-start(bf16[256,256]{1,0:T(8,128)(2,1)S(1)} %get-tuple-element.32), channel_id=1, source_target_pairs={{0,2},{1,5},{2,0},{3,7},{4,6},{5,1},{6,4},{7,3},{8,10},{9,13},{10,... | collective-permute-start | bytes 393224 | tf_op jit(solution)/shard_map/ppermute | solution.py:170
  33.3 6.0 %copy-start = (bf16[512,512]{1,0:T(8,128)(2,1)S(1)}, bf16[512,512]{1,0:T(8,128)(2,1)}, u32[]{:S(2)}) copy-start(bf16[512,512]{1,0:T(8,128)(2,1)} %refs_6_.1) | copy-start | bytes 1572868
  33.3 5.9 %collective-permute-start.13 = (bf16[256,256]{1,0:T(8,128)(2,1)S(1)}, bf16[256,256]{1,0:T(8,128)(2,1)S(1)}, u32[]{:S(2)}, u32[]{:S(2)}) collective-permute-start(bf16[256,256]{1,0:T(8,128)(2,1)S(1)} %shard_map.75), channel_id=1, source_target_pairs={{0,4},{1,3},{2,6},{3,1},{4,0},{5,7},{6,2},{7,5},{8,12},{9,11},{10,... | collective-permute-start | bytes 393224 | tf_op jit(solution)/shard_map/ppermute | solution.py:170
where the time goes:
time: 40.6 us; the launch traced here: 40.3 us
  waiting for transfers between devices  18.4 us (45%)
  starting transfers between devices  11.9 us (29%)
  Pallas kernels  8.47 us (21%)
  between operations  0.81 us (2%)
  local copies, waits for them, and re-layouts  0.65 us (2%)
    ppermute x6, waiting for transfers between devices, exchange_chips(): lax.ppermute(x, 'col', [(j, j ^ (far if j & 1 else near)) for j in range(...  17.2 us
    pallas_call x13, Pallas kernels, call(): pl.pallas_call(kernel, out_shape=outs, in_specs=specs or [vmem] * len(ins...  8.47 us
    ppermute x8, starting transfers between devices, exchange(): lax.ppermute(x, axis, [(i, i ^ distance) for i in range(lax.axis_size(axi...  7.54 us
    ppermute x6, starting transfers between devices, exchange_chips(): lax.ppermute(x, 'col', [(j, j ^ (far if j & 1 else near)) for j in range(...  4.38 us
    ppermute x8, waiting for transfers between devices, exchange(): lax.ppermute(x, axis, [(i, i ^ distance) for i in range(lax.axis_size(axi...  1.2 us
  transfers between devices with their start and end apart: 14, of which 4 were waited for; matrix products, arithmetic and copies ran while one was open for 0% of the time, Pallas kernels for 16%

commit v1 on v0

--- a/solution.py
+++ b/solution.py
@@ -32,11 +32,11 @@
     return jnp.where(core == 0, near, slot >> 1)
 
 
-def tile_kernel(bits, rows, shard, order_hbm, blocks_hbm, count_ref, slots_ref, give_ref, keep_ref, pick_ref,
-                order_ref, blocks_ref, sems):
+def tile_kernel(bits, rows, shard, order_hbm, blocks_hbm, slots_hbm, count_ref, give_ref, keep_ref, pick_ref,
+                order_ref, blocks_ref, slots_ref, sems):
     copies = [
         pltpu.make_async_copy(src, dst, sems.at[k])
-        for k, (src, dst) in enumerate(((order_hbm, order_ref), (blocks_hbm, blocks_ref)))
+        for k, (src, dst) in enumerate(((order_hbm, order_ref), (blocks_hbm, blocks_ref), (slots_hbm, slots_ref)))
     ]
     for copy in copies:
         copy.start()
@@ -57,6 +57,7 @@
         column = nodes[:, k * (width // colblk):k * (width // colblk) + 1]
         pick_ref[k * width:(k + 1) * width, :] = jnp.where(corpus == column, 1.0, 0.0).astype(pick_ref.dtype)
     copies[1].wait()
+    copies[2].wait()
 
     def step(index, carry):
         code = slots_ref[0, 0, index]
@@ -114,19 +115,16 @@
     hold_ref[...] = mine_ref[:hold_ref.shape[0], :] + got_ref[...].astype(jnp.float32)
 
 
-def project_kernel(*refs):
-    weight_ref, out_ref = refs[-2], refs[-1]
-    projected, start = None, 0
-    for part in range((len(refs) - 2) // 3):
-        mine_ref, near_ref, far_ref = refs[3 * part:3 * part + 3]
-        total = mine_ref[:near_ref.shape[0], :] + near_ref[...].astype(jnp.float32) + far_ref[...].astype(jnp.float32)
-        depth = total.shape[1]
-        product = jnp.dot(
-            total.astype(jnp.bfloat16), weight_ref[start:start + depth, :], preferred_element_type=jnp.float32
-        )
-        projected = product if projected is None else projected + product
-        start += depth
-    out_ref[...] = jnp.maximum(projected, 0.0).astype(out_ref.dtype)
+def project_kernel(start, first, last, *refs):
+    mine_ref, near_ref, far_ref, weight_ref = refs[:4]
+    before, out_ref = refs[4:-1], refs[-1]
+    total = mine_ref[:near_ref.shape[0], :] + near_ref[...].astype(jnp.float32) + far_ref[...].astype(jnp.float32)
+    projected = jnp.dot(
+        total.astype(jnp.bfloat16), weight_ref[start:start + total.shape[1], :], preferred_element_type=jnp.float32
+    )
+    if not first:
+        projected += before[0][...]
+    out_ref[...] = (jnp.maximum(projected, 0.0) if last else projected).astype(out_ref.dtype)
 
 
 def per_device(features, order, tile_count, tile_slots, blocks, weight):
@@ -174,19 +172,24 @@
         cut_kernel, [shape((shard, depth), bf16) for depth in widths], [in_hbm(features)],
         [hbm], [pltpu.SemaphoreType.DMA((len(widths),))], 1,
     )
-    gathered = [[mine] + [exchange(mine, "row", k) for k in range(1, rows_axis)] for mine in cuts]
     table = (group // width, width)
     give, keep, pick = call(
         functools.partial(tile_kernel, bits, rows, shard),
         [shape((half * rows, group), bf16)] * 2 + [shape((group, group), bf16)],
-        [in_hbm(order.reshape(table)), in_hbm(blocks), tile_count, tile_slots],
-        [hbm, hbm, smem, smem],
+        [in_hbm(order.reshape(table)), in_hbm(blocks), in_hbm(tile_slots), tile_count],
+        [hbm, hbm, hbm, smem],
         [
             pltpu.VMEM(table, jnp.int32),
             pltpu.VMEM(blocks.shape, bf16),
-            pltpu.SemaphoreType.DMA((2,)),
+            pltpu.SMEM(tile_slots.shape, jnp.int32),
+            pltpu.SemaphoreType.DMA((3,)),
         ],
     )
+
+    gathered = []
+    for mine in cuts:
+        mine = after(mine, give) if gathered else mine
+        gathered.append([mine] + [exchange(mine, "row", k) for k in range(1, rows_axis)])
 
     def pieces(count, depth):
         return [shape((count // 2 * rows, depth), bf16)] * 2 if count > 1 else [shape((rows, depth), bf16)]
@@ -209,7 +212,7 @@
             low, high = [exchange_chips(send, step) for send in sends]
             step += 1
 
-    ends, waiting, sent, lows = [], None, [], []
+    ends, waiting, sent = [], None, []
     for features, depth in zip(gathered, widths, strict=True):
         if waiting is not None:
             features = [after(features[0], waiting[0]), *features[1:]]
@@ -221,9 +224,19 @@
             ordered = after(ordered, sent[0])
         mine = call(sum_kernel, shape((half * rows, depth), f32), [keep, ordered])
         waiting = first_step(mine, got)
-        lows.append(waiting[2])
-    ends += later_steps(waiting[0], after(waiting[1], *lows[:-1], *ends[2::3]), waiting[2])
-    return call(project_kernel, shape((rows, feats), bf16), [*ends, weight])
+    ends += later_steps(waiting[0], after(waiting[1], *ends[1::3], *ends[2::3]), waiting[2])
+    projected, start = [], 0
+    for k, depth in enumerate(widths):
+        first, last = k == 0, k == len(widths) - 1
+        terms = ends[3 * k:3 * k + 3]
+        if not last:
+            terms[0] = after(terms[0], sent[0])
+        projected = [call(
+            functools.partial(project_kernel, start, first, last), shape((rows, feats), bf16 if last else f32),
+            [*terms, weight, *projected], cost=1,
+        )]
+        start += depth
+    return projected[0]
 
 
 def solution(mesh):

time: 40.6 us -> 39.5 us (0.973)
  the two profiles are of different devices: /device:TPU:30 before, /device:TPU:0 now
where the time goes in v1:
time: 39.5 us; the launch traced here: 39.6 us
  starting transfers between devices  18.1 us (46%)
  waiting for transfers between devices  12.3 us (31%)
  Pallas kernels  8.4 us (21%)
  between operations  0.77 us (2%)
    ppermute x6, waiting for transfers between devices, exchange_chips(): lax.ppermute(x, 'col', [(j, j ^ (far if j & 1 else near)) for j in range(...  10.3 us
    ppermute x8, starting transfers between devices, exchange(): lax.ppermute(x, axis, [(i, i ^ distance) for i in range(lax.axis_size(axi...  9.44 us
    ppermute x6, starting transfers between devices, exchange_chips(): lax.ppermute(x, 'col', [(j, j ^ (far if j & 1 else near)) for j in range(...  8.7 us
    pallas_call x14, Pallas kernels, call(): pl.pallas_call(kernel, out_shape=outs, in_specs=specs or [vmem] * len(ins...  8.4 us
    ppermute x8, waiting for transfers between devices, exchange(): lax.ppermute(x, axis, [(i, i ^ distance) for i in range(lax.axis_size(axi...  2 us
  transfers between devices with their start and end apart: 14, of which 8 were waited for; matrix products, arithmetic and copies ran while one was open for 0% of the time, Pallas kernels for 16%

profile of v1, /device:TPU:0, one launch (start us, length us, event | category | flops | bytes accessed | tf_op | source)
XLA Modules:
  0.0 39.6 jit_solution(15313319285438220518)
XLA Ops:
  0.0 1.0 %shard_map.65 = (bf16[256,256]{1,0:T(8,128)(2,1)S(1)}, bf16[256,256]{1,0:T(8,128)(2,1)S(1)}) custom-call(bf16[256,512]{1,0:T(8,128)(2,1)} %x_hbm.1), custom_call_target="tpu_custom_call" | custom-call | flops 1 | bytes 1 | tf_op jit(solution)/shard_map/pallas_call | solution.py:146
  1.0 3.0 %collective-permute-start = (bf16[256,256]{1,0:T(8,128)(2,1)S(1)}, bf16[256,256]{1,0:T(8,128)(2,1)S(1)}, u32[]{:S(2)}, u32[]{:S(2)}) collective-permute-start(bf16[256,256]{1,0:T(8,128)(2,1)S(1)} %get-tuple-element.27.refs_0_), channel_id=1, source_target_pairs={{0,8},{8,0},{16,24},{24,16},{1,9},{9,1},{17,25},{25,17},{2,10},{10... | collective-permute-start | bytes 393224 | tf_op jit(solution)/shard_map/ppermute | solution.py:163
  4.0 1.5 %collective-permute-start.1 = (bf16[256,256]{1,0:T(8,128)(2,1)S(1)}, bf16[256,256]{1,0:T(8,128)(2,1)S(1)}, u32[]{:S(2)}, u32[]{:S(2)}) collective-permute-start(bf16[256,256]{1,0:T(8,128)(2,1)S(1)} %get-tuple-element.27.refs_0_), channel_id=1, source_target_pairs={{0,16},{8,24},{16,0},{24,8},{1,17},{9,25},{17,1},{25,9},{2,18},{10... | collective-permute-start | bytes 393224 | tf_op jit(solution)/shard_map/ppermute | solution.py:163
  6.2 1.8 %shard_map.64 = (bf16[1024,1024]{1,0:T(8,128)(2,1)S(1)}, bf16[1024,1024]{1,0:T(8,128)(2,1)S(1)}, bf16[1024,1024]{1,0:T(8,128)(2,1)S(1)}) custom-call(s32[8,128]{1,0:T(8,128)} %bitcast.1, bf16[1,1,16,128,128]{4,3,2,1,0:T(8,128)(2,1)} %blocks_hbm.1, s32[1,1,16]{2,1,0:T(1,128)} %slots_hbm.1, s32[1,1]{1,0:T(1,128)S(6)} %copy.7.count_ref), custom_call_target="tpu_custom_call" | custom-call | flops 10000000000 | bytes 10000000000 | tf_op jit(solution)/shard_map/pallas_call | solution.py:146
  8.0 1.5 %collective-permute-start.4 = (bf16[256,256]{1,0:T(8,128)(2,1)S(1)}, bf16[256,256]{1,0:T(8,128)(2,1)S(1)}, u32[]{:S(2)}, u32[]{:S(2)}) collective-permute-start(bf16[256,256]{1,0:T(8,128)(2,1)S(1)} %get-tuple-element.29.refs_0_), channel_id=1, source_target_pairs={{0,8},{8,0},{16,24},{24,16},{1,9},{9,1},{17,25},{25,17},{2,10},{10... | collective-permute-start | bytes 393224 | tf_op jit(solution)/shard_map/ppermute | solution.py:163
  9.5 1.7 %collective-permute-start.5 = (bf16[256,256]{1,0:T(8,128)(2,1)S(1)}, bf16[256,256]{1,0:T(8,128)(2,1)S(1)}, u32[]{:S(2)}, u32[]{:S(2)}) collective-permute-start(bf16[256,256]{1,0:T(8,128)(2,1)S(1)} %get-tuple-element.29.refs_0_), channel_id=1, source_target_pairs={{0,16},{8,24},{16,0},{24,8},{1,17},{9,25},{17,1},{25,9},{2,18},{10... | collective-permute-start | bytes 393224 | tf_op jit(solution)/shard_map/ppermute | solution.py:163
  11.6 0.8 %collective-permute-done.2.refs_3_ = bf16[256,256]{1,0:T(8,128)(2,1)S(1)} collective-permute-done((bf16[256,256]{1,0:T(8,128)(2,1)S(1)}, bf16[256,256]{1,0:T(8,128)(2,1)S(1)}, u32[]{:S(2)}, u32[]{:S(2)}) %collective-permute-start.2) | collective-permute-done | bytes 131104 | tf_op jit(solution)/shard_map/ppermute | solution.py:163
  12.4 0.7 %shard_map.66.ordered_ref = bf16[1024,256]{1,0:T(8,128)(2,1)S(1)} custom-call(bf16[1024,1024]{1,0:T(8,128)(2,1)S(1)} %get-tuple-element.23.pick_ref, bf16[256,256]{1,0:T(8,128)(2,1)S(1)} %get-tuple-element.27.refs_0_, bf16[256,256]{1,0:T(8,128)(2,1)S(1)} %collective-permute-done.refs_1_, bf16[256,256]{1,0:T(8,128)(2,1)S(1)} %collective-permute-done.1.refs_2_, ...), custom_call_target="tpu_custom_call" | custom-call | flops 10000000000 | bytes 10000000000 | tf_op jit(solution)/shard_map/pallas_call | solution.py:146
  13.1 0.7 %shard_map.68 = bf16[1024,256]{1,0:T(8,128)(2,1)S(1)} custom-call(bf16[1024,1024]{1,0:T(8,128)(2,1)S(1)} %get-tuple-element.25.tile_ref, bf16[1024,256]{1,0:T(8,128)(2,1)S(1)} %shard_map.66.ordered_ref), custom_call_target="tpu_custom_call" | custom-call | flops 10000000000 | bytes 10000000000 | tf_op jit(solution)/shard_map/pallas_call | solution.py:146
  13.9 0.7 %shard_map.67.mine_ref = f32[1024,256]{1,0:T(8,128)S(1)} custom-call(bf16[1024,1024]{1,0:T(8,128)(2,1)S(1)} %get-tuple-element.22.tile_ref, bf16[1024,256]{1,0:T(8,128)(2,1)S(1)} %shard_map.66.ordered_ref), custom_call_target="tpu_custom_call" | custom-call | flops 10000000000 | bytes 10000000000 | tf_op jit(solution)/shard_map/pallas_call | solution.py:146
  14.6 1.2 %collective-permute-done.3.got_ref = bf16[1024,256]{1,0:T(8,128)(2,1)S(1)} collective-permute-done((bf16[1024,256]{1,0:T(8,128)(2,1)S(1)}, bf16[1024,256]{1,0:T(8,128)(2,1)S(1)}, u32[]{:S(2)}, u32[]{:S(2)}) %collective-permute-start.3) | collective-permute-done | bytes 524320 | tf_op jit(solution)/shard_map/ppermute | solution.py:163
  15.9 1.6 %collective-permute-start.7 = (bf16[256,256]{1,0:T(8,128)(2,1)S(1)}, bf16[256,256]{1,0:T(8,128)(2,1)S(1)}, u32[]{:S(2)}, u32[]{:S(2)}) collective-permute-start(bf16[256,256]{1,0:T(8,128)(2,1)S(1)} %get-tuple-element.30), channel_id=1, source_target_pairs={{0,2},{1,5},{2,0},{3,7},{4,6},{5,1},{6,4},{7,3},{8,10},{9,13},{10,... | collective-permute-start | bytes 393224 | tf_op jit(solution)/shard_map/ppermute | solution.py:168
  17.4 0.7 %shard_map.70.ordered_ref = bf16[1024,256]{1,0:T(8,128)(2,1)S(1)} custom-call(bf16[1024,1024]{1,0:T(8,128)(2,1)S(1)} %get-tuple-element.23.pick_ref, bf16[256,256]{1,0:T(8,128)(2,1)S(1)} %get-tuple-element.29.refs_0_, bf16[256,256]{1,0:T(8,128)(2,1)S(1)} %collective-permute-done.4.refs_1_, bf16[256,256]{1,0:T(8,128)(2,1)S(1)} %collective-permute-done.5.refs_2_, ...), custom_call_target="tpu_custom_call" | custom-call | flops 10000000000 | bytes 10000000000 | tf_op jit(solution)/shard_map/pallas_call | solution.py:146
  18.2 0.7 %shard_map.71 = bf16[1024,256]{1,0:T(8,128)(2,1)S(1)} custom-call(bf16[1024,1024]{1,0:T(8,128)(2,1)S(1)} %get-tuple-element.25.tile_ref, bf16[1024,256]{1,0:T(8,128)(2,1)S(1)} %shard_map.70.ordered_ref), custom_call_target="tpu_custom_call" | custom-call | flops 10000000000 | bytes 10000000000 | tf_op jit(solution)/shard_map/pallas_call | solution.py:146
  18.9 1.3 %collective-permute-start.8 = (bf16[1024,256]{1,0:T(8,128)(2,1)S(1)}, bf16[1024,256]{1,0:T(8,128)(2,1)S(1)}, u32[]{:S(2)}, u32[]{:S(2)}) collective-permute-start(bf16[1024,256]{1,0:T(8,128)(2,1)S(1)} %shard_map.71), channel_id=1, source_target_pairs={{0,1},{1,0},{2,3},{3,2},{4,5},{5,4},{6,7},{7,6},{8,9},{9,8},{10,11... | collective-permute-start | bytes 1572872 | tf_op jit(solution)/shard_map/ppermute | solution.py:163
  20.1 1.2 %collective-permute-start.11 = (bf16[256,256]{1,0:T(8,128)(2,1)S(1)}, bf16[256,256]{1,0:T(8,128)(2,1)S(1)}, u32[]{:S(2)}, u32[]{:S(2)}) collective-permute-start(bf16[256,256]{1,0:T(8,128)(2,1)S(1)} %get-tuple-element.36), channel_id=1, source_target_pairs={{0,2},{1,5},{2,0},{3,7},{4,6},{5,1},{6,4},{7,3},{8,10},{9,13},{10,... | collective-permute-start | bytes 393224 | tf_op jit(solution)/shard_map/ppermute | solution.py:168
  21.7 2.3 %collective-permute-start.12 = (bf16[256,256]{1,0:T(8,128)(2,1)S(1)}, bf16[256,256]{1,0:T(8,128)(2,1)S(1)}, u32[]{:S(2)}, u32[]{:S(2)}) collective-permute-start(bf16[256,256]{1,0:T(8,128)(2,1)S(1)} %shard_map.72), channel_id=1, source_target_pairs={{0,4},{1,3},{2,6},{3,1},{4,0},{5,7},{6,2},{7,5},{8,12},{9,11},{10,... | collective-permute-start | bytes 393224 | tf_op jit(solution)/shard_map/ppermute | solution.py:168
  24.8 2.3 %collective-permute-start.10 = (bf16[256,256]{1,0:T(8,128)(2,1)S(1)}, bf16[256,256]{1,0:T(8,128)(2,1)S(1)}, u32[]{:S(2)}, u32[]{:S(2)}) collective-permute-start(bf16[256,256]{1,0:T(8,128)(2,1)S(1)} %get-tuple-element.35), channel_id=1, source_target_pairs={{0,2},{1,5},{2,0},{3,7},{4,6},{5,1},{6,4},{7,3},{8,10},{9,13},{10,... | collective-permute-start | bytes 393224 | tf_op jit(solution)/shard_map/ppermute | solution.py:168
  27.2 1.8 %collective-permute-done.11.refs_1_ = bf16[256,256]{1,0:T(8,128)(2,1)S(1)} collective-permute-done((bf16[256,256]{1,0:T(8,128)(2,1)S(1)}, bf16[256,256]{1,0:T(8,128)(2,1)S(1)}, u32[]{:S(2)}, u32[]{:S(2)}) %collective-permute-start.11) | collective-permute-done | bytes 131104 | tf_op jit(solution)/shard_map/ppermute | solution.py:168
  29.3 3.0 %collective-permute-done.10.got_ref = bf16[256,256]{1,0:T(8,128)(2,1)S(1)} collective-permute-done((bf16[256,256]{1,0:T(8,128)(2,1)S(1)}, bf16[256,256]{1,0:T(8,128)(2,1)S(1)}, u32[]{:S(2)}, u32[]{:S(2)}) %collective-permute-start.10) | collective-permute-done | bytes 131104 | tf_op jit(solution)/shard_map/ppermute | solution.py:168
  32.4 1.3 %collective-permute-start.13 = (bf16[256,256]{1,0:T(8,128)(2,1)S(1)}, bf16[256,256]{1,0:T(8,128)(2,1)S(1)}, u32[]{:S(2)}, u32[]{:S(2)}) collective-permute-start(bf16[256,256]{1,0:T(8,128)(2,1)S(1)} %shard_map.75), channel_id=1, source_target_pairs={{0,4},{1,3},{2,6},{3,1},{4,0},{5,7},{6,2},{7,5},{8,12},{9,11},{10,... | collective-permute-start | bytes 393224 | tf_op jit(solution)/shard_map/ppermute | solution.py:168
  33.9 1.2 %collective-permute-done.9.refs_1_ = bf16[256,256]{1,0:T(8,128)(2,1)S(1)} collective-permute-done((bf16[256,256]{1,0:T(8,128)(2,1)S(1)}, bf16[256,256]{1,0:T(8,128)(2,1)S(1)}, u32[]{:S(2)}, u32[]{:S(2)}) %collective-permute-start.9) | collective-permute-done | bytes 131104 | tf_op jit(solution)/shard_map/ppermute | solution.py:168
  35.2 3.5 %collective-permute-done.13.refs_2_ = bf16[256,256]{1,0:T(8,128)(2,1)S(1)} collective-permute-done((bf16[256,256]{1,0:T(8,128)(2,1)S(1)}, bf16[256,256]{1,0:T(8,128)(2,1)S(1)}, u32[]{:S(2)}, u32[]{:S(2)}) %collective-permute-start.13) | collective-permute-done | bytes 131104 | tf_op jit(solution)/shard_map/ppermute | solution.py:168
  38.7 0.9 %shard_map.77 = bf16[256,512]{1,0:T(8,128)(2,1)} custom-call(f32[512,256]{1,0:T(8,128)S(1)} %get-tuple-element.33.mine_ref.refs_0_, bf16[256,256]{1,0:T(8,128)(2,1)S(1)} %collective-permute-done.9.refs_1_, bf16[256,256]{1,0:T(8,128)(2,1)S(1)} %collective-permute-done.13.refs_2_, bf16[512,512]{1,0:T(8,128)(2,1)S(1)} %copy-done, f32[256,512]{1,0:T(8,128)S(1)} %shard_map.76.refs_4_), custom_call_target="tpu_custom_call" | custom-call | flops 1 | bytes 1 | tf_op jit(solution)/shard_map/pallas_call | solution.py:146
  (20 shorter events, 2.4 us)
Async XLA Ops:
  1.0 10.2 %collective-permute-start = (bf16[256,256]{1,0:T(8,128)(2,1)S(1)}, bf16[256,256]{1,0:T(8,128)(2,1)S(1)}, u32[]{:S(2)}, u32[]{:S(2)}) collective-permute-start(bf16[256,256]{1,0:T(8,128)(2,1)S(1)} %get-tuple-element.27.refs_0_), channel_id=1, source_target_pairs={{0,8},{8,0},{16,24},{24,16},{1,9},{9,1},{17,25},{25,17},{2,10},{10... | collective-permute-start | bytes 393224 | tf_op jit(solution)/shard_map/ppermute | solution.py:163
  4.0 7.6 %collective-permute-start.1 = (bf16[256,256]{1,0:T(8,128)(2,1)S(1)}, bf16[256,256]{1,0:T(8,128)(2,1)S(1)}, u32[]{:S(2)}, u32[]{:S(2)}) collective-permute-start(bf16[256,256]{1,0:T(8,128)(2,1)S(1)} %get-tuple-element.27.refs_0_), channel_id=1, source_target_pairs={{0,16},{8,24},{16,0},{24,8},{1,17},{9,25},{17,1},{25,9},{2,18},{10... | collective-permute-start | bytes 393224 | tf_op jit(solution)/shard_map/ppermute | solution.py:163
  5.5 6.8 %collective-permute-start.2 = (bf16[256,256]{1,0:T(8,128)(2,1)S(1)}, bf16[256,256]{1,0:T(8,128)(2,1)S(1)}, u32[]{:S(2)}, u32[]{:S(2)}) collective-permute-start(bf16[256,256]{1,0:T(8,128)(2,1)S(1)} %get-tuple-element.27.refs_0_), channel_id=1, source_target_pairs={{0,24},{8,16},{16,8},{24,0},{1,25},{9,17},{17,9},{25,1},{2,26},{10... | collective-permute-start | bytes 393224 | tf_op jit(solution)/shard_map/ppermute | solution.py:163
  8.0 9.4 %collective-permute-start.4 = (bf16[256,256]{1,0:T(8,128)(2,1)S(1)}, bf16[256,256]{1,0:T(8,128)(2,1)S(1)}, u32[]{:S(2)}, u32[]{:S(2)}) collective-permute-start(bf16[256,256]{1,0:T(8,128)(2,1)S(1)} %get-tuple-element.29.refs_0_), channel_id=1, source_target_pairs={{0,8},{8,0},{16,24},{24,16},{1,9},{9,1},{17,25},{25,17},{2,10},{10... | collective-permute-start | bytes 393224 | tf_op jit(solution)/shard_map/ppermute | solution.py:163
  9.5 7.9 %collective-permute-start.5 = (bf16[256,256]{1,0:T(8,128)(2,1)S(1)}, bf16[256,256]{1,0:T(8,128)(2,1)S(1)}, u32[]{:S(2)}, u32[]{:S(2)}) collective-permute-start(bf16[256,256]{1,0:T(8,128)(2,1)S(1)} %get-tuple-element.29.refs_0_), channel_id=1, source_target_pairs={{0,16},{8,24},{16,0},{24,8},{1,17},{9,25},{17,1},{25,9},{2,18},{10... | collective-permute-start | bytes 393224 | tf_op jit(solution)/shard_map/ppermute | solution.py:163
  11.2 6.2 %collective-permute-start.6 = (bf16[256,256]{1,0:T(8,128)(2,1)S(1)}, bf16[256,256]{1,0:T(8,128)(2,1)S(1)}, u32[]{:S(2)}, u32[]{:S(2)}) collective-permute-start(bf16[256,256]{1,0:T(8,128)(2,1)S(1)} %get-tuple-element.29.refs_0_), channel_id=1, source_target_pairs={{0,24},{8,16},{16,8},{24,0},{1,25},{9,17},{17,9},{25,1},{2,26},{10... | collective-permute-start | bytes 393224 | tf_op jit(solution)/shard_map/ppermute | solution.py:163
  13.8 2.0 %collective-permute-start.3 = (bf16[1024,256]{1,0:T(8,128)(2,1)S(1)}, bf16[1024,256]{1,0:T(8,128)(2,1)S(1)}, u32[]{:S(2)}, u32[]{:S(2)}) collective-permute-start(bf16[1024,256]{1,0:T(8,128)(2,1)S(1)} %shard_map.68), channel_id=1, source_target_pairs={{0,1},{1,0},{2,3},{3,2},{4,5},{5,4},{6,7},{7,6},{8,9},{9,8},{10,11... | collective-permute-start | bytes 1572872 | tf_op jit(solution)/shard_map/ppermute | solution.py:163
  15.9 5.9 %collective-permute-start.7 = (bf16[256,256]{1,0:T(8,128)(2,1)S(1)}, bf16[256,256]{1,0:T(8,128)(2,1)S(1)}, u32[]{:S(2)}, u32[]{:S(2)}) collective-permute-start(bf16[256,256]{1,0:T(8,128)(2,1)S(1)} %get-tuple-element.30), channel_id=1, source_target_pairs={{0,2},{1,5},{2,0},{3,7},{4,6},{5,1},{6,4},{7,3},{8,10},{9,13},{10,... | collective-permute-start | bytes 393224 | tf_op jit(solution)/shard_map/ppermute | solution.py:168
  18.9 5.9 %collective-permute-start.8 = (bf16[1024,256]{1,0:T(8,128)(2,1)S(1)}, bf16[1024,256]{1,0:T(8,128)(2,1)S(1)}, u32[]{:S(2)}, u32[]{:S(2)}) collective-permute-start(bf16[1024,256]{1,0:T(8,128)(2,1)S(1)} %shard_map.71), channel_id=1, source_target_pairs={{0,1},{1,0},{2,3},{3,2},{4,5},{5,4},{6,7},{7,6},{8,9},{9,8},{10,11... | collective-permute-start | bytes 1572872 | tf_op jit(solution)/shard_map/ppermute | solution.py:163
  20.1 8.8 %collective-permute-start.11 = (bf16[256,256]{1,0:T(8,128)(2,1)S(1)}, bf16[256,256]{1,0:T(8,128)(2,1)S(1)}, u32[]{:S(2)}, u32[]{:S(2)}) collective-permute-start(bf16[256,256]{1,0:T(8,128)(2,1)S(1)} %get-tuple-element.36), channel_id=1, source_target_pairs={{0,2},{1,5},{2,0},{3,7},{4,6},{5,1},{6,4},{7,3},{8,10},{9,13},{10,... | collective-permute-start | bytes 393224 | tf_op jit(solution)/shard_map/ppermute | solution.py:168
  21.7 7.6 %collective-permute-start.12 = (bf16[256,256]{1,0:T(8,128)(2,1)S(1)}, bf16[256,256]{1,0:T(8,128)(2,1)S(1)}, u32[]{:S(2)}, u32[]{:S(2)}) collective-permute-start(bf16[256,256]{1,0:T(8,128)(2,1)S(1)} %shard_map.72), channel_id=1, source_target_pairs={{0,4},{1,3},{2,6},{3,1},{4,0},{5,7},{6,2},{7,5},{8,12},{9,11},{10,... | collective-permute-start | bytes 393224 | tf_op jit(solution)/shard_map/ppermute | solution.py:168
  24.8 7.5 %collective-permute-start.10 = (bf16[256,256]{1,0:T(8,128)(2,1)S(1)}, bf16[256,256]{1,0:T(8,128)(2,1)S(1)}, u32[]{:S(2)}, u32[]{:S(2)}) collective-permute-start(bf16[256,256]{1,0:T(8,128)(2,1)S(1)} %get-tuple-element.35), channel_id=1, source_target_pairs={{0,2},{1,5},{2,0},{3,7},{4,6},{5,1},{6,4},{7,3},{8,10},{9,13},{10,... | collective-permute-start | bytes 393224 | tf_op jit(solution)/shard_map/ppermute | solution.py:168
  27.1 8.1 %collective-permute-start.9 = (bf16[256,256]{1,0:T(8,128)(2,1)S(1)}, bf16[256,256]{1,0:T(8,128)(2,1)S(1)}, u32[]{:S(2)}, u32[]{:S(2)}) collective-permute-start(bf16[256,256]{1,0:T(8,128)(2,1)S(1)} %get-tuple-element.34), channel_id=1, source_target_pairs={{0,2},{1,5},{2,0},{3,7},{4,6},{5,1},{6,4},{7,3},{8,10},{9,13},{10,... | collective-permute-start | bytes 393224 | tf_op jit(solution)/shard_map/ppermute | solution.py:168
  32.4 1.3 %copy-start = (bf16[512,512]{1,0:T(8,128)(2,1)S(1)}, bf16[512,512]{1,0:T(8,128)(2,1)}, u32[]{:S(2)}) copy-start(bf16[512,512]{1,0:T(8,128)(2,1)} %refs_3_.3) | copy-start | bytes 1572868
  32.4 6.3 %collective-permute-start.13 = (bf16[256,256]{1,0:T(8,128)(2,1)S(1)}, bf16[256,256]{1,0:T(8,128)(2,1)S(1)}, u32[]{:S(2)}, u32[]{:S(2)}) collective-permute-start(bf16[256,256]{1,0:T(8,128)(2,1)S(1)} %shard_map.75), channel_id=1, source_target_pairs={{0,4},{1,3},{2,6},{3,1},{4,0},{5,7},{6,2},{7,5},{8,12},{9,11},{10,... | collective-permute-start | bytes 393224 | tf_op jit(solution)/shard_map/ppermute | solution.py:168

commit v2 on v1

--- a/solution.py
+++ b/solution.py
@@ -10,6 +10,7 @@
 VMEM_LIMIT = 16 * 1024 * 1024
 SHARES = (1, 1)
 COST = 10**10
+OUT_PIECES = 2
 
 
 def cut_kernel(x_hbm, *refs):
@@ -117,14 +118,30 @@
 
 def project_kernel(start, first, last, *refs):
     mine_ref, near_ref, far_ref, weight_ref = refs[:4]
-    before, out_ref = refs[4:-1], refs[-1]
-    total = mine_ref[:near_ref.shape[0], :] + near_ref[...].astype(jnp.float32) + far_ref[...].astype(jnp.float32)
-    projected = jnp.dot(
-        total.astype(jnp.bfloat16), weight_ref[start:start + total.shape[1], :], preferred_element_type=jnp.float32
-    )
-    if not first:
-        projected += before[0][...]
-    out_ref[...] = (jnp.maximum(projected, 0.0) if last else projected).astype(out_ref.dtype)
+    before, out_ref = (refs[4:5], refs[5]) if not first else ((), refs[4])
+    rows = far_ref.shape[0]
+    weight = weight_ref[start:start + far_ref.shape[1], :]
+
+    def some(here):
+        total = mine_ref[here, :] + near_ref[here, :].astype(jnp.float32) + far_ref[here, :].astype(jnp.float32)
+        projected = jnp.dot(total.astype(jnp.bfloat16), weight, preferred_element_type=jnp.float32)
+        return projected if first else projected + before[0][here, :]
+
+    if not last:
+        out_ref[...] = some(slice(0, rows))
+        return
+    held_ref, sems = refs[-2], refs[-1]
+    count = rows // OUT_PIECES
+    copies = []
+    for k in range(OUT_PIECES):
+        here = slice(k * count, (k + 1) * count)
+        held_ref[here, :] = jnp.maximum(some(here), 0.0).astype(held_ref.dtype)
+        copies.append(pltpu.make_async_copy(
+            held_ref.at[pl.ds(k * count, count), :], out_ref.at[pl.ds(k * count, count), :], sems.at[k]
+        ))
+        copies[-1].start()
+    for copy in copies:
+        copy.wait()
 
 
 def per_device(features, order, tile_count, tile_slots, blocks, weight):
@@ -142,12 +159,12 @@
     bf16, f32 = jnp.bfloat16, jnp.float32
     shape = jax.ShapeDtypeStruct
 
-    def call(kernel, outs, ins, specs=None, scratch=(), cost=COST):
+    def call(kernel, outs, ins, specs=None, scratch=(), cost=COST, out_hbm=False):
         return pl.pallas_call(
             kernel,
             out_shape=outs,
             in_specs=specs or [vmem] * len(ins),
-            out_specs=jax.tree.map(lambda _: vmem, outs),
+            out_specs=jax.tree.map(lambda _: hbm if out_hbm else vmem, outs),
             scratch_shapes=scratch,
             compiler_params=params,
             cost_estimate=pl.CostEstimate(flops=cost, bytes_accessed=cost, transcendentals=0),
@@ -233,7 +250,8 @@
             terms[0] = after(terms[0], sent[0])
         projected = [call(
             functools.partial(project_kernel, start, first, last), shape((rows, feats), bf16 if last else f32),
-            [*terms, weight, *projected], cost=1,
+            [*terms, weight, *projected], cost=1, out_hbm=last,
+            scratch=[pltpu.VMEM((rows, feats), bf16), pltpu.SemaphoreType.DMA((OUT_PIECES,))] if last else (),
         )]
         start += depth
     return projected[0]

time: 39.5 us -> 39.5 us (level)
  the two profiles are of different devices: /device:TPU:0 before, /device:TPU:8 now
where the time goes in v2:
time: 39.5 us; the launch traced here: 39.2 us
  starting transfers between devices  18 us (46%)
  waiting for transfers between devices  12.5 us (32%)
  Pallas kernels  7.87 us (20%)
  between operations  0.78 us (2%)
    ppermute x6, starting transfers between devices, exchange_chips(): lax.ppermute(x, 'col', [(j, j ^ (far if j & 1 else near)) for j in range(...  9.74 us
    ppermute x6, waiting for transfers between devices, exchange_chips(): lax.ppermute(x, 'col', [(j, j ^ (far if j & 1 else near)) for j in range(...  9.54 us
    ppermute x8, starting transfers between devices, exchange(): lax.ppermute(x, axis, [(i, i ^ distance) for i in range(lax.axis_size(axi...  8.28 us
    pallas_call x14, Pallas kernels, call(): pl.pallas_call(kernel, out_shape=outs, in_specs=specs or [vmem] * len(ins...  7.87 us
    ppermute x8, waiting for transfers between devices, exchange(): lax.ppermute(x, axis, [(i, i ^ distance) for i in range(lax.axis_size(axi...  3.01 us
  transfers between devices with their start and end apart: 14, of which 7 were waited for; matrix products, arithmetic and copies ran while one was open for 0% of the time, Pallas kernels for 15%

profile of v2, /device:TPU:8, one launch (start us, length us, event | category | flops | bytes accessed | tf_op | source)
XLA Modules:
  0.0 39.2 jit_solution(6831407577010215055)
XLA Ops:
  0.0 1.0 %shard_map.65 = (bf16[256,256]{1,0:T(8,128)(2,1)S(1)}, bf16[256,256]{1,0:T(8,128)(2,1)S(1)}) custom-call(bf16[256,512]{1,0:T(8,128)(2,1)} %x_hbm.1), custom_call_target="tpu_custom_call" | custom-call | flops 1 | bytes 1 | tf_op jit(solution)/shard_map/pallas_call | solution.py:163
  1.0 1.6 %collective-permute-start = (bf16[256,256]{1,0:T(8,128)(2,1)S(1)}, bf16[256,256]{1,0:T(8,128)(2,1)S(1)}, u32[]{:S(2)}, u32[]{:S(2)}) collective-permute-start(bf16[256,256]{1,0:T(8,128)(2,1)S(1)} %get-tuple-element.27.refs_0_), channel_id=1, source_target_pairs={{0,8},{8,0},{16,24},{24,16},{1,9},{9,1},{17,25},{25,17},{2,10},{10... | collective-permute-start | bytes 393224 | tf_op jit(solution)/shard_map/ppermute | solution.py:180
  2.5 1.5 %collective-permute-start.1 = (bf16[256,256]{1,0:T(8,128)(2,1)S(1)}, bf16[256,256]{1,0:T(8,128)(2,1)S(1)}, u32[]{:S(2)}, u32[]{:S(2)}) collective-permute-start(bf16[256,256]{1,0:T(8,128)(2,1)S(1)} %get-tuple-element.27.refs_0_), channel_id=1, source_target_pairs={{0,16},{8,24},{16,0},{24,8},{1,17},{9,25},{17,1},{25,9},{2,18},{10... | collective-permute-start | bytes 393224 | tf_op jit(solution)/shard_map/ppermute | solution.py:180
  5.2 1.3 %shard_map.64 = (bf16[1024,1024]{1,0:T(8,128)(2,1)S(1)}, bf16[1024,1024]{1,0:T(8,128)(2,1)S(1)}, bf16[1024,1024]{1,0:T(8,128)(2,1)S(1)}) custom-call(s32[8,128]{1,0:T(8,128)} %bitcast.1, bf16[1,1,16,128,128]{4,3,2,1,0:T(8,128)(2,1)} %blocks_hbm.1, s32[1,1,16]{2,1,0:T(1,128)} %slots_hbm.1, s32[1,1]{1,0:T(1,128)S(6)} %copy.7.count_ref), custom_call_target="tpu_custom_call" | custom-call | flops 10000000000 | bytes 10000000000 | tf_op jit(solution)/shard_map/pallas_call | solution.py:163
  6.5 1.6 %collective-permute-start.4 = (bf16[256,256]{1,0:T(8,128)(2,1)S(1)}, bf16[256,256]{1,0:T(8,128)(2,1)S(1)}, u32[]{:S(2)}, u32[]{:S(2)}) collective-permute-start(bf16[256,256]{1,0:T(8,128)(2,1)S(1)} %get-tuple-element.29.refs_0_), channel_id=1, source_target_pairs={{0,8},{8,0},{16,24},{24,16},{1,9},{9,1},{17,25},{25,17},{2,10},{10... | collective-permute-start | bytes 393224 | tf_op jit(solution)/shard_map/ppermute | solution.py:180
  8.1 1.6 %collective-permute-start.5 = (bf16[256,256]{1,0:T(8,128)(2,1)S(1)}, bf16[256,256]{1,0:T(8,128)(2,1)S(1)}, u32[]{:S(2)}, u32[]{:S(2)}) collective-permute-start(bf16[256,256]{1,0:T(8,128)(2,1)S(1)} %get-tuple-element.29.refs_0_), channel_id=1, source_target_pairs={{0,16},{8,24},{16,0},{24,8},{1,17},{9,25},{17,1},{25,9},{2,18},{10... | collective-permute-start | bytes 393224 | tf_op jit(solution)/shard_map/ppermute | solution.py:180
  10.0 1.0 %collective-permute-done.2.refs_3_ = bf16[256,256]{1,0:T(8,128)(2,1)S(1)} collective-permute-done((bf16[256,256]{1,0:T(8,128)(2,1)S(1)}, bf16[256,256]{1,0:T(8,128)(2,1)S(1)}, u32[]{:S(2)}, u32[]{:S(2)}) %collective-permute-start.2) | collective-permute-done | bytes 131104 | tf_op jit(solution)/shard_map/ppermute | solution.py:180
  11.1 0.7 %shard_map.66.ordered_ref = bf16[1024,256]{1,0:T(8,128)(2,1)S(1)} custom-call(bf16[1024,1024]{1,0:T(8,128)(2,1)S(1)} %get-tuple-element.23.pick_ref, bf16[256,256]{1,0:T(8,128)(2,1)S(1)} %get-tuple-element.27.refs_0_, bf16[256,256]{1,0:T(8,128)(2,1)S(1)} %collective-permute-done.refs_1_, bf16[256,256]{1,0:T(8,128)(2,1)S(1)} %collective-permute-done.1.refs_2_, ...), custom_call_target="tpu_custom_call" | custom-call | flops 10000000000 | bytes 10000000000 | tf_op jit(solution)/shard_map/pallas_call | solution.py:163
  11.8 0.7 %shard_map.68 = bf16[1024,256]{1,0:T(8,128)(2,1)S(1)} custom-call(bf16[1024,1024]{1,0:T(8,128)(2,1)S(1)} %get-tuple-element.25.tile_ref, bf16[1024,256]{1,0:T(8,128)(2,1)S(1)} %shard_map.66.ordered_ref), custom_call_target="tpu_custom_call" | custom-call | flops 10000000000 | bytes 10000000000 | tf_op jit(solution)/shard_map/pallas_call | solution.py:163
  12.6 0.7 %shard_map.67.mine_ref = f32[1024,256]{1,0:T(8,128)S(1)} custom-call(bf16[1024,1024]{1,0:T(8,128)(2,1)S(1)} %get-tuple-element.22.tile_ref, bf16[1024,256]{1,0:T(8,128)(2,1)S(1)} %shard_map.66.ordered_ref), custom_call_target="tpu_custom_call" | custom-call | flops 10000000000 | bytes 10000000000 | tf_op jit(solution)/shard_map/pallas_call | solution.py:163
  13.3 1.2 %collective-permute-done.3.got_ref = bf16[1024,256]{1,0:T(8,128)(2,1)S(1)} collective-permute-done((bf16[1024,256]{1,0:T(8,128)(2,1)S(1)}, bf16[1024,256]{1,0:T(8,128)(2,1)S(1)}, u32[]{:S(2)}, u32[]{:S(2)}) %collective-permute-start.3) | collective-permute-done | bytes 524320 | tf_op jit(solution)/shard_map/ppermute | solution.py:180
  15.2 0.8 %collective-permute-done.5.refs_2_ = bf16[256,256]{1,0:T(8,128)(2,1)S(1)} collective-permute-done((bf16[256,256]{1,0:T(8,128)(2,1)S(1)}, bf16[256,256]{1,0:T(8,128)(2,1)S(1)}, u32[]{:S(2)}, u32[]{:S(2)}) %collective-permute-start.5) | collective-permute-done | bytes 131104 | tf_op jit(solution)/shard_map/ppermute | solution.py:180
  16.0 0.7 %shard_map.70.ordered_ref = bf16[1024,256]{1,0:T(8,128)(2,1)S(1)} custom-call(bf16[1024,1024]{1,0:T(8,128)(2,1)S(1)} %get-tuple-element.23.pick_ref, bf16[256,256]{1,0:T(8,128)(2,1)S(1)} %get-tuple-element.29.refs_0_, bf16[256,256]{1,0:T(8,128)(2,1)S(1)} %collective-permute-done.4.refs_1_, bf16[256,256]{1,0:T(8,128)(2,1)S(1)} %collective-permute-done.5.refs_2_, ...), custom_call_target="tpu_custom_call" | custom-call | flops 10000000000 | bytes 10000000000 | tf_op jit(solution)/shard_map/pallas_call | solution.py:163
  16.7 0.7 %shard_map.71 = bf16[1024,256]{1,0:T(8,128)(2,1)S(1)} custom-call(bf16[1024,1024]{1,0:T(8,128)(2,1)S(1)} %get-tuple-element.25.tile_ref, bf16[1024,256]{1,0:T(8,128)(2,1)S(1)} %shard_map.70.ordered_ref), custom_call_target="tpu_custom_call" | custom-call | flops 10000000000 | bytes 10000000000 | tf_op jit(solution)/shard_map/pallas_call | solution.py:163
  17.4 1.1 %collective-permute-start.8 = (bf16[1024,256]{1,0:T(8,128)(2,1)S(1)}, bf16[1024,256]{1,0:T(8,128)(2,1)S(1)}, u32[]{:S(2)}, u32[]{:S(2)}) collective-permute-start(bf16[1024,256]{1,0:T(8,128)(2,1)S(1)} %shard_map.71), channel_id=1, source_target_pairs={{0,1},{1,0},{2,3},{3,2},{4,5},{5,4},{6,7},{7,6},{8,9},{9,8},{10,11... | collective-permute-start | bytes 1572872 | tf_op jit(solution)/shard_map/ppermute | solution.py:180
  18.5 0.6 %collective-permute-start.11 = (bf16[256,256]{1,0:T(8,128)(2,1)S(1)}, bf16[256,256]{1,0:T(8,128)(2,1)S(1)}, u32[]{:S(2)}, u32[]{:S(2)}) collective-permute-start(bf16[256,256]{1,0:T(8,128)(2,1)S(1)} %get-tuple-element.36), channel_id=1, source_target_pairs={{0,2},{1,5},{2,0},{3,7},{4,6},{5,1},{6,4},{7,3},{8,10},{9,13},{10,... | collective-permute-start | bytes 393224 | tf_op jit(solution)/shard_map/ppermute | solution.py:185
  19.2 1.6 %collective-permute-done.7.got_ref = bf16[256,256]{1,0:T(8,128)(2,1)S(1)} collective-permute-done((bf16[256,256]{1,0:T(8,128)(2,1)S(1)}, bf16[256,256]{1,0:T(8,128)(2,1)S(1)}, u32[]{:S(2)}, u32[]{:S(2)}) %collective-permute-start.7) | collective-permute-done | bytes 131104 | tf_op jit(solution)/shard_map/ppermute | solution.py:185
  20.8 2.8 %collective-permute-start.12 = (bf16[256,256]{1,0:T(8,128)(2,1)S(1)}, bf16[256,256]{1,0:T(8,128)(2,1)S(1)}, u32[]{:S(2)}, u32[]{:S(2)}) collective-permute-start(bf16[256,256]{1,0:T(8,128)(2,1)S(1)} %shard_map.72), channel_id=1, source_target_pairs={{0,4},{1,3},{2,6},{3,1},{4,0},{5,7},{6,2},{7,5},{8,12},{9,11},{10,... | collective-permute-start | bytes 393224 | tf_op jit(solution)/shard_map/ppermute | solution.py:185
  23.5 0.7 %shard_map.73.mine_ref = f32[1024,256]{1,0:T(8,128)S(1)} custom-call(bf16[1024,1024]{1,0:T(8,128)(2,1)S(1)} %get-tuple-element.22.tile_ref, bf16[1024,256]{1,0:T(8,128)(2,1)S(1)} %shard_map.70.ordered_ref), custom_call_target="tpu_custom_call" | custom-call | flops 10000000000 | bytes 10000000000 | tf_op jit(solution)/shard_map/pallas_call | solution.py:163
  24.4 2.0 %collective-permute-start.9 = (bf16[256,256]{1,0:T(8,128)(2,1)S(1)}, bf16[256,256]{1,0:T(8,128)(2,1)S(1)}, u32[]{:S(2)}, u32[]{:S(2)}) collective-permute-start(bf16[256,256]{1,0:T(8,128)(2,1)S(1)} %get-tuple-element.34), channel_id=1, source_target_pairs={{0,2},{1,5},{2,0},{3,7},{4,6},{5,1},{6,4},{7,3},{8,10},{9,13},{10,... | collective-permute-start | bytes 393224 | tf_op jit(solution)/shard_map/ppermute | solution.py:185
  26.4 4.1 %collective-permute-done.12.refs_2_ = bf16[256,256]{1,0:T(8,128)(2,1)S(1)} collective-permute-done((bf16[256,256]{1,0:T(8,128)(2,1)S(1)}, bf16[256,256]{1,0:T(8,128)(2,1)S(1)}, u32[]{:S(2)}, u32[]{:S(2)}) %collective-permute-start.12) | collective-permute-done | bytes 131104 | tf_op jit(solution)/shard_map/ppermute | solution.py:185
  30.9 3.6 %collective-permute-start.13 = (bf16[256,256]{1,0:T(8,128)(2,1)S(1)}, bf16[256,256]{1,0:T(8,128)(2,1)S(1)}, u32[]{:S(2)}, u32[]{:S(2)}) collective-permute-start(bf16[256,256]{1,0:T(8,128)(2,1)S(1)} %shard_map.75), channel_id=1, source_target_pairs={{0,4},{1,3},{2,6},{3,1},{4,0},{5,7},{6,2},{7,5},{8,12},{9,11},{10,... | collective-permute-start | bytes 393224 | tf_op jit(solution)/shard_map/ppermute | solution.py:185
  34.8 3.5 %collective-permute-done.13.refs_2_ = bf16[256,256]{1,0:T(8,128)(2,1)S(1)} collective-permute-done((bf16[256,256]{1,0:T(8,128)(2,1)S(1)}, bf16[256,256]{1,0:T(8,128)(2,1)S(1)}, u32[]{:S(2)}, u32[]{:S(2)}) %collective-permute-start.13) | collective-permute-done | bytes 131104 | tf_op jit(solution)/shard_map/ppermute | solution.py:185
  38.3 0.9 %shard_map.77 = bf16[256,512]{1,0:T(8,128)(2,1)} custom-call(f32[512,256]{1,0:T(8,128)S(1)} %get-tuple-element.33.mine_ref.refs_0_, bf16[256,256]{1,0:T(8,128)(2,1)S(1)} %collective-permute-done.9.refs_1_, bf16[256,256]{1,0:T(8,128)(2,1)S(1)} %collective-permute-done.13.refs_2_, bf16[512,512]{1,0:T(8,128)(2,1)S(1)} %copy-done, f32[256,512]{1,0:T(8,128)S(1)} %shard_map.76.refs_4_), custom_call_target="tpu_custom_call" | custom-call | flops 1 | bytes 1 | tf_op jit(solution)/shard_map/pallas_call | solution.py:163
  (20 shorter events, 2.3 us)
Async XLA Ops:
  1.0 8.8 %collective-permute-start = (bf16[256,256]{1,0:T(8,128)(2,1)S(1)}, bf16[256,256]{1,0:T(8,128)(2,1)S(1)}, u32[]{:S(2)}, u32[]{:S(2)}) collective-permute-start(bf16[256,256]{1,0:T(8,128)(2,1)S(1)} %get-tuple-element.27.refs_0_), channel_id=1, source_target_pairs={{0,8},{8,0},{16,24},{24,16},{1,9},{9,1},{17,25},{25,17},{2,10},{10... | collective-permute-start | bytes 393224 | tf_op jit(solution)/shard_map/ppermute | solution.py:180
  2.5 7.5 %collective-permute-start.1 = (bf16[256,256]{1,0:T(8,128)(2,1)S(1)}, bf16[256,256]{1,0:T(8,128)(2,1)S(1)}, u32[]{:S(2)}, u32[]{:S(2)}) collective-permute-start(bf16[256,256]{1,0:T(8,128)(2,1)S(1)} %get-tuple-element.27.refs_0_), channel_id=1, source_target_pairs={{0,16},{8,24},{16,0},{24,8},{1,17},{9,25},{17,1},{25,9},{2,18},{10... | collective-permute-start | bytes 393224 | tf_op jit(solution)/shard_map/ppermute | solution.py:180
  4.1 7.0 %collective-permute-start.2 = (bf16[256,256]{1,0:T(8,128)(2,1)S(1)}, bf16[256,256]{1,0:T(8,128)(2,1)S(1)}, u32[]{:S(2)}, u32[]{:S(2)}) collective-permute-start(bf16[256,256]{1,0:T(8,128)(2,1)S(1)} %get-tuple-element.27.refs_0_), channel_id=1, source_target_pairs={{0,24},{8,16},{16,8},{24,0},{1,25},{9,17},{17,9},{25,1},{2,26},{10... | collective-permute-start | bytes 393224 | tf_op jit(solution)/shard_map/ppermute | solution.py:180
  6.5 8.7 %collective-permute-start.4 = (bf16[256,256]{1,0:T(8,128)(2,1)S(1)}, bf16[256,256]{1,0:T(8,128)(2,1)S(1)}, u32[]{:S(2)}, u32[]{:S(2)}) collective-permute-start(bf16[256,256]{1,0:T(8,128)(2,1)S(1)} %get-tuple-element.29.refs_0_), channel_id=1, source_target_pairs={{0,8},{8,0},{16,24},{24,16},{1,9},{9,1},{17,25},{25,17},{2,10},{10... | collective-permute-start | bytes 393224 | tf_op jit(solution)/shard_map/ppermute | solution.py:180
  8.1 7.9 %collective-permute-start.5 = (bf16[256,256]{1,0:T(8,128)(2,1)S(1)}, bf16[256,256]{1,0:T(8,128)(2,1)S(1)}, u32[]{:S(2)}, u32[]{:S(2)}) collective-permute-start(bf16[256,256]{1,0:T(8,128)(2,1)S(1)} %get-tuple-element.29.refs_0_), channel_id=1, source_target_pairs={{0,16},{8,24},{16,0},{24,8},{1,17},{9,25},{17,1},{25,9},{2,18},{10... | collective-permute-start | bytes 393224 | tf_op jit(solution)/shard_map/ppermute | solution.py:180
  9.8 6.2 %collective-permute-start.6 = (bf16[256,256]{1,0:T(8,128)(2,1)S(1)}, bf16[256,256]{1,0:T(8,128)(2,1)S(1)}, u32[]{:S(2)}, u32[]{:S(2)}) collective-permute-start(bf16[256,256]{1,0:T(8,128)(2,1)S(1)} %get-tuple-element.29.refs_0_), channel_id=1, source_target_pairs={{0,24},{8,16},{16,8},{24,0},{1,25},{9,17},{17,9},{25,1},{2,26},{10... | collective-permute-start | bytes 393224 | tf_op jit(solution)/shard_map/ppermute | solution.py:180
  12.5 2.0 %collective-permute-start.3 = (bf16[1024,256]{1,0:T(8,128)(2,1)S(1)}, bf16[1024,256]{1,0:T(8,128)(2,1)S(1)}, u32[]{:S(2)}, u32[]{:S(2)}) collective-permute-start(bf16[1024,256]{1,0:T(8,128)(2,1)S(1)} %shard_map.68), channel_id=1, source_target_pairs={{0,1},{1,0},{2,3},{3,2},{4,5},{5,4},{6,7},{7,6},{8,9},{9,8},{10,11... | collective-permute-start | bytes 1572872 | tf_op jit(solution)/shard_map/ppermute | solution.py:180
  14.6 6.1 %collective-permute-start.7 = (bf16[256,256]{1,0:T(8,128)(2,1)S(1)}, bf16[256,256]{1,0:T(8,128)(2,1)S(1)}, u32[]{:S(2)}, u32[]{:S(2)}) collective-permute-start(bf16[256,256]{1,0:T(8,128)(2,1)S(1)} %get-tuple-element.30), channel_id=1, source_target_pairs={{0,2},{1,5},{2,0},{3,7},{4,6},{5,1},{6,4},{7,3},{8,10},{9,13},{10,... | collective-permute-start | bytes 393224 | tf_op jit(solution)/shard_map/ppermute | solution.py:185
  17.4 6.8 %collective-permute-start.8 = (bf16[1024,256]{1,0:T(8,128)(2,1)S(1)}, bf16[1024,256]{1,0:T(8,128)(2,1)S(1)}, u32[]{:S(2)}, u32[]{:S(2)}) collective-permute-start(bf16[1024,256]{1,0:T(8,128)(2,1)S(1)} %shard_map.71), channel_id=1, source_target_pairs={{0,1},{1,0},{2,3},{3,2},{4,5},{5,4},{6,7},{7,6},{8,9},{9,8},{10,11... | collective-permute-start | bytes 1572872 | tf_op jit(solution)/shard_map/ppermute | solution.py:180
  18.5 7.9 %collective-permute-start.11 = (bf16[256,256]{1,0:T(8,128)(2,1)S(1)}, bf16[256,256]{1,0:T(8,128)(2,1)S(1)}, u32[]{:S(2)}, u32[]{:S(2)}) collective-permute-start(bf16[256,256]{1,0:T(8,128)(2,1)S(1)} %get-tuple-element.36), channel_id=1, source_target_pairs={{0,2},{1,5},{2,0},{3,7},{4,6},{5,1},{6,4},{7,3},{8,10},{9,13},{10,... | collective-permute-start | bytes 393224 | tf_op jit(solution)/shard_map/ppermute | solution.py:185
  20.8 9.8 %collective-permute-start.12 = (bf16[256,256]{1,0:T(8,128)(2,1)S(1)}, bf16[256,256]{1,0:T(8,128)(2,1)S(1)}, u32[]{:S(2)}, u32[]{:S(2)}) collective-permute-start(bf16[256,256]{1,0:T(8,128)(2,1)S(1)} %shard_map.72), channel_id=1, source_target_pairs={{0,4},{1,3},{2,6},{3,1},{4,0},{5,7},{6,2},{7,5},{8,12},{9,11},{10,... | collective-permute-start | bytes 393224 | tf_op jit(solution)/shard_map/ppermute | solution.py:185
  24.3 6.5 %collective-permute-start.10 = (bf16[256,256]{1,0:T(8,128)(2,1)S(1)}, bf16[256,256]{1,0:T(8,128)(2,1)S(1)}, u32[]{:S(2)}, u32[]{:S(2)}) collective-permute-start(bf16[256,256]{1,0:T(8,128)(2,1)S(1)} %get-tuple-element.35), channel_id=1, source_target_pairs={{0,2},{1,5},{2,0},{3,7},{4,6},{5,1},{6,4},{7,3},{8,10},{9,13},{10,... | collective-permute-start | bytes 393224 | tf_op jit(solution)/shard_map/ppermute | solution.py:185
  24.4 10.3 %collective-permute-start.9 = (bf16[256,256]{1,0:T(8,128)(2,1)S(1)}, bf16[256,256]{1,0:T(8,128)(2,1)S(1)}, u32[]{:S(2)}, u32[]{:S(2)}) collective-permute-start(bf16[256,256]{1,0:T(8,128)(2,1)S(1)} %get-tuple-element.34), channel_id=1, source_target_pairs={{0,2},{1,5},{2,0},{3,7},{4,6},{5,1},{6,4},{7,3},{8,10},{9,13},{10,... | collective-permute-start | bytes 393224 | tf_op jit(solution)/shard_map/ppermute | solution.py:185
  30.9 3.7 %copy-start = (bf16[512,512]{1,0:T(8,128)(2,1)S(1)}, bf16[512,512]{1,0:T(8,128)(2,1)}, u32[]{:S(2)}) copy-start(bf16[512,512]{1,0:T(8,128)(2,1)} %refs_3_.3) | copy-start | bytes 1572868
  30.9 7.4 %collective-permute-start.13 = (bf16[256,256]{1,0:T(8,128)(2,1)S(1)}, bf16[256,256]{1,0:T(8,128)(2,1)S(1)}, u32[]{:S(2)}, u32[]{:S(2)}) collective-permute-start(bf16[256,256]{1,0:T(8,128)(2,1)S(1)} %shard_map.75), channel_id=1, source_target_pairs={{0,4},{1,3},{2,6},{3,1},{4,0},{5,7},{6,2},{7,5},{8,12},{9,11},{10,... | collective-permute-start | bytes 393224 | tf_op jit(solution)/shard_map/ppermute | solution.py:185

commit v3 on v1

--- a/solution.py
+++ b/solution.py
@@ -12,17 +12,10 @@
 COST = 10**10
 
 
-def cut_kernel(x_hbm, *refs):
-    outs, sems = refs[:-1], refs[-1]
-    copies, start = [], 0
-    for k, out in enumerate(outs):
-        depth = out.shape[1]
-        copies.append(pltpu.make_async_copy(x_hbm.at[:, pl.ds(start, depth)], out, sems.at[k]))
-        start += depth
-    for copy in copies:
-        copy.start()
-    for copy in copies:
-        copy.wait()
+def cut_kernel(start, x_hbm, out_ref, sem):
+    copy = pltpu.make_async_copy(x_hbm.at[:, pl.ds(start, out_ref.shape[1])], out_ref, sem)
+    copy.start()
+    copy.wait()
 
 
 def place_of(slot, core, bits):
@@ -32,11 +25,13 @@
     return jnp.where(core == 0, near, slot >> 1)
 
 
-def tile_kernel(bits, rows, shard, order_hbm, blocks_hbm, slots_hbm, count_ref, give_ref, keep_ref, pick_ref,
-                order_ref, blocks_ref, slots_ref, sems):
+def tile_kernel(bits, rows, shard, order_hbm, blocks_hbm, slots_hbm, x_hbm, count_ref, give_ref, keep_ref, pick_ref,
+                cut_ref, order_ref, blocks_ref, slots_ref, sems):
     copies = [
         pltpu.make_async_copy(src, dst, sems.at[k])
-        for k, (src, dst) in enumerate(((order_hbm, order_ref), (blocks_hbm, blocks_ref), (slots_hbm, slots_ref)))
+        for k, (src, dst) in enumerate(((order_hbm, order_ref), (blocks_hbm, blocks_ref), (slots_hbm, slots_ref), (
+            x_hbm.at[:, pl.ds(x_hbm.shape[1] - cut_ref.shape[1], cut_ref.shape[1])], cut_ref,
+        )))
     ]
     for copy in copies:
         copy.start()
@@ -58,6 +53,7 @@
         pick_ref[k * width:(k + 1) * width, :] = jnp.where(corpus == column, 1.0, 0.0).astype(pick_ref.dtype)
     copies[1].wait()
     copies[2].wait()
+    copies[3].wait()
 
     def step(index, carry):
         code = slots_ref[0, 0, index]
@@ -168,23 +164,28 @@
         return lax.ppermute(x, "col", [(j, j ^ (far if j & 1 else near)) for j in range(cols_axis)])
 
     widths = [feats * share // sum(SHARES) for share in SHARES]
-    cuts = call(
-        cut_kernel, [shape((shard, depth), bf16) for depth in widths], [in_hbm(features)],
-        [hbm], [pltpu.SemaphoreType.DMA((len(widths),))], 1,
-    )
+    cuts, start = [], 0
+    for depth in widths[:-1]:
+        cuts.append(call(
+            functools.partial(cut_kernel, start), shape((shard, depth), bf16), [in_hbm(features)],
+            [hbm], [pltpu.SemaphoreType.DMA], 1,
+        ))
+        start += depth
     table = (group // width, width)
-    give, keep, pick = call(
+    give, keep, pick, cut = call(
         functools.partial(tile_kernel, bits, rows, shard),
-        [shape((half * rows, group), bf16)] * 2 + [shape((group, group), bf16)],
-        [in_hbm(order.reshape(table)), in_hbm(blocks), in_hbm(tile_slots), tile_count],
-        [hbm, hbm, hbm, smem],
+        [shape((half * rows, group), bf16)] * 2
+        + [shape((group, group), bf16), shape((shard, widths[-1]), bf16)],
+        [in_hbm(order.reshape(table)), in_hbm(blocks), in_hbm(tile_slots), in_hbm(features), tile_count],
+        [hbm, hbm, hbm, hbm, smem],
         [
             pltpu.VMEM(table, jnp.int32),
             pltpu.VMEM(blocks.shape, bf16),
             pltpu.SMEM(tile_slots.shape, jnp.int32),
-            pltpu.SemaphoreType.DMA((3,)),
+            pltpu.SemaphoreType.DMA((4,)),
         ],
     )
+    cuts.append(cut)
 
     gathered = []
     for mine in cuts:

time: 39.5 us -> 39.1 us (0.990)
  the two profiles are of different devices: /device:TPU:0 before, /device:TPU:24 now
where the time goes in v3:
time: 39.1 us; the launch traced here: 38.9 us
  waiting for transfers between devices  18.8 us (48%)
  starting transfers between devices  10.5 us (27%)
  Pallas kernels  7.86 us (20%)
  local copies, waits for them, and re-layouts  0.93 us (2%)
  between operations  0.8 us (2%)
    ppermute x6, waiting for transfers between devices, exchange_chips(): lax.ppermute(x, 'col', [(j, j ^ (far if j & 1 else near)) for j in range(...  15.6 us
    pallas_call x14, Pallas kernels, call(): pl.pallas_call(kernel, out_shape=outs, in_specs=specs or [vmem] * len(ins...  7.86 us
    ppermute x8, starting transfers between devices, exchange(): lax.ppermute(x, axis, [(i, i ^ distance) for i in range(lax.axis_size(axi...  7.25 us
    ppermute x6, starting transfers between devices, exchange_chips(): lax.ppermute(x, 'col', [(j, j ^ (far if j & 1 else near)) for j in range(...  3.24 us
    ppermute x8, waiting for transfers between devices, exchange(): lax.ppermute(x, axis, [(i, i ^ distance) for i in range(lax.axis_size(axi...  3.21 us
    unnamed x2, local copies, waits for them, and re-layouts  0.93 us
  transfers between devices with their start and end apart: 14, of which 7 were waited for; matrix products, arithmetic and copies ran while one was open for 0% of the time, Pallas kernels for 15%

profile of v3, /device:TPU:24, one launch (start us, length us, event | category | flops | bytes accessed | tf_op | source)
XLA Modules:
  0.0 38.9 jit_solution(5399800771173894237)
XLA Ops:
  0.0 0.9 %shard_map.65.refs_0_ = bf16[256,256]{1,0:T(8,128)(2,1)S(1)} custom-call(bf16[256,512]{1,0:T(8,128)(2,1)} %x_hbm.3), custom_call_target="tpu_custom_call" | custom-call | flops 1 | bytes 1 | tf_op jit(solution)/shard_map/pallas_call | solution.py:142
  0.9 1.6 %collective-permute-start = (bf16[256,256]{1,0:T(8,128)(2,1)S(1)}, bf16[256,256]{1,0:T(8,128)(2,1)S(1)}, u32[]{:S(2)}, u32[]{:S(2)}) collective-permute-start(bf16[256,256]{1,0:T(8,128)(2,1)S(1)} %shard_map.65.refs_0_), channel_id=1, source_target_pairs={{0,8},{8,0},{16,24},{24,16},{1,9},{9,1},{17,25},{25,17},{2,10},{10... | collective-permute-start | bytes 393224 | tf_op jit(solution)/shard_map/ppermute | solution.py:159
  2.5 1.5 %collective-permute-start.1 = (bf16[256,256]{1,0:T(8,128)(2,1)S(1)}, bf16[256,256]{1,0:T(8,128)(2,1)S(1)}, u32[]{:S(2)}, u32[]{:S(2)}) collective-permute-start(bf16[256,256]{1,0:T(8,128)(2,1)S(1)} %shard_map.65.refs_0_), channel_id=1, source_target_pairs={{0,16},{8,24},{16,0},{24,8},{1,17},{9,25},{17,1},{25,9},{2,18},{10... | collective-permute-start | bytes 393224 | tf_op jit(solution)/shard_map/ppermute | solution.py:159
  4.0 0.5 %collective-permute-start.2 = (bf16[256,256]{1,0:T(8,128)(2,1)S(1)}, bf16[256,256]{1,0:T(8,128)(2,1)S(1)}, u32[]{:S(2)}, u32[]{:S(2)}) collective-permute-start(bf16[256,256]{1,0:T(8,128)(2,1)S(1)} %shard_map.65.refs_0_), channel_id=1, source_target_pairs={{0,24},{8,16},{16,8},{24,0},{1,25},{9,17},{17,9},{25,1},{2,26},{10... | collective-permute-start | bytes 393224 | tf_op jit(solution)/shard_map/ppermute | solution.py:159
  5.1 1.3 %shard_map.64 = (bf16[1024,1024]{1,0:T(8,128)(2,1)S(1)}, bf16[1024,1024]{1,0:T(8,128)(2,1)S(1)}, bf16[1024,1024]{1,0:T(8,128)(2,1)S(1)}, bf16[256,256]{1,0:T(8,128)(2,1)S(1)}) custom-call(s32[8,128]{1,0:T(8,128)} %bitcast.1, bf16[1,1,16,128,128]{4,3,2,1,0:T(8,128)(2,1)} %blocks_hbm.1, s32[1,1,16]{2,1,0:T(1,128)} %slots_hbm.1, bf16[256,512]{1,0:T(8,128)(2,1)} %x_hbm.3, ...), custom_call_target="tpu_custom_call" | custom-call | flops 10000000000 | bytes 10000000000 | tf_op jit(solution)/shard_map/pallas_call | solution.py:142
  6.5 1.6 %collective-permute-start.4 = (bf16[256,256]{1,0:T(8,128)(2,1)S(1)}, bf16[256,256]{1,0:T(8,128)(2,1)S(1)}, u32[]{:S(2)}, u32[]{:S(2)}) collective-permute-start(bf16[256,256]{1,0:T(8,128)(2,1)S(1)} %get-tuple-element.27.refs_0_), channel_id=1, source_target_pairs={{0,8},{8,0},{16,24},{24,16},{1,9},{9,1},{17,25},{25,17},{2,10},{10... | collective-permute-start | bytes 393224 | tf_op jit(solution)/shard_map/ppermute | solution.py:159
  8.1 1.9 %collective-permute-start.5 = (bf16[256,256]{1,0:T(8,128)(2,1)S(1)}, bf16[256,256]{1,0:T(8,128)(2,1)S(1)}, u32[]{:S(2)}, u32[]{:S(2)}) collective-permute-start(bf16[256,256]{1,0:T(8,128)(2,1)S(1)} %get-tuple-element.27.refs_0_), channel_id=1, source_target_pairs={{0,16},{8,24},{16,0},{24,8},{1,17},{9,25},{17,1},{25,9},{2,18},{10... | collective-permute-start | bytes 393224 | tf_op jit(solution)/shard_map/ppermute | solution.py:159
  10.0 0.9 %collective-permute-done.2.refs_3_ = bf16[256,256]{1,0:T(8,128)(2,1)S(1)} collective-permute-done((bf16[256,256]{1,0:T(8,128)(2,1)S(1)}, bf16[256,256]{1,0:T(8,128)(2,1)S(1)}, u32[]{:S(2)}, u32[]{:S(2)}) %collective-permute-start.2) | collective-permute-done | bytes 131104 | tf_op jit(solution)/shard_map/ppermute | solution.py:159
  10.9 0.7 %shard_map.66.ordered_ref = bf16[1024,256]{1,0:T(8,128)(2,1)S(1)} custom-call(bf16[1024,1024]{1,0:T(8,128)(2,1)S(1)} %get-tuple-element.22.pick_ref, bf16[256,256]{1,0:T(8,128)(2,1)S(1)} %shard_map.65.refs_0_, bf16[256,256]{1,0:T(8,128)(2,1)S(1)} %collective-permute-done.refs_1_, bf16[256,256]{1,0:T(8,128)(2,1)S(1)} %collective-permute-done.1.refs_2_, ...), custom_call_target="tpu_custom_call" | custom-call | flops 10000000000 | bytes 10000000000 | tf_op jit(solution)/shard_map/pallas_call | solution.py:142
  11.6 0.7 %shard_map.68 = bf16[1024,256]{1,0:T(8,128)(2,1)S(1)} custom-call(bf16[1024,1024]{1,0:T(8,128)(2,1)S(1)} %get-tuple-element.24.tile_ref, bf16[1024,256]{1,0:T(8,128)(2,1)S(1)} %shard_map.66.ordered_ref), custom_call_target="tpu_custom_call" | custom-call | flops 10000000000 | bytes 10000000000 | tf_op jit(solution)/shard_map/pallas_call | solution.py:142
  12.4 0.7 %shard_map.67.mine_ref = f32[1024,256]{1,0:T(8,128)S(1)} custom-call(bf16[1024,1024]{1,0:T(8,128)(2,1)S(1)} %get-tuple-element.21.tile_ref, bf16[1024,256]{1,0:T(8,128)(2,1)S(1)} %shard_map.66.ordered_ref), custom_call_target="tpu_custom_call" | custom-call | flops 10000000000 | bytes 10000000000 | tf_op jit(solution)/shard_map/pallas_call | solution.py:142
  13.1 1.2 %collective-permute-done.3.got_ref = bf16[1024,256]{1,0:T(8,128)(2,1)S(1)} collective-permute-done((bf16[1024,256]{1,0:T(8,128)(2,1)S(1)}, bf16[1024,256]{1,0:T(8,128)(2,1)S(1)}, u32[]{:S(2)}, u32[]{:S(2)}) %collective-permute-start.3) | collective-permute-done | bytes 524320 | tf_op jit(solution)/shard_map/ppermute | solution.py:159
  14.9 1.0 %collective-permute-done.6.refs_3_ = bf16[256,256]{1,0:T(8,128)(2,1)S(1)} collective-permute-done((bf16[256,256]{1,0:T(8,128)(2,1)S(1)}, bf16[256,256]{1,0:T(8,128)(2,1)S(1)}, u32[]{:S(2)}, u32[]{:S(2)}) %collective-permute-start.6) | collective-permute-done | bytes 131104 | tf_op jit(solution)/shard_map/ppermute | solution.py:159
  15.9 0.7 %shard_map.70.ordered_ref = bf16[1024,256]{1,0:T(8,128)(2,1)S(1)} custom-call(bf16[1024,1024]{1,0:T(8,128)(2,1)S(1)} %get-tuple-element.22.pick_ref, bf16[256,256]{1,0:T(8,128)(2,1)S(1)} %get-tuple-element.27.refs_0_, bf16[256,256]{1,0:T(8,128)(2,1)S(1)} %collective-permute-done.4.refs_1_, bf16[256,256]{1,0:T(8,128)(2,1)S(1)} %collective-permute-done.5.refs_2_, ...), custom_call_target="tpu_custom_call" | custom-call | flops 10000000000 | bytes 10000000000 | tf_op jit(solution)/shard_map/pallas_call | solution.py:142
  16.6 0.7 %shard_map.71 = bf16[1024,256]{1,0:T(8,128)(2,1)S(1)} custom-call(bf16[1024,1024]{1,0:T(8,128)(2,1)S(1)} %get-tuple-element.24.tile_ref, bf16[1024,256]{1,0:T(8,128)(2,1)S(1)} %shard_map.70.ordered_ref), custom_call_target="tpu_custom_call" | custom-call | flops 10000000000 | bytes 10000000000 | tf_op jit(solution)/shard_map/pallas_call | solution.py:142
  17.4 0.7 %collective-permute-start.11 = (bf16[256,256]{1,0:T(8,128)(2,1)S(1)}, bf16[256,256]{1,0:T(8,128)(2,1)S(1)}, u32[]{:S(2)}, u32[]{:S(2)}) collective-permute-start(bf16[256,256]{1,0:T(8,128)(2,1)S(1)} %get-tuple-element.34), channel_id=1, source_target_pairs={{0,2},{1,5},{2,0},{3,7},{4,6},{5,1},{6,4},{7,3},{8,10},{9,13},{10,... | collective-permute-start | bytes 393224 | tf_op jit(solution)/shard_map/ppermute | solution.py:164
  18.1 2.8 %collective-permute-done.7.got_ref = bf16[256,256]{1,0:T(8,128)(2,1)S(1)} collective-permute-done((bf16[256,256]{1,0:T(8,128)(2,1)S(1)}, bf16[256,256]{1,0:T(8,128)(2,1)S(1)}, u32[]{:S(2)}, u32[]{:S(2)}) %collective-permute-start.7) | collective-permute-done | bytes 131104 | tf_op jit(solution)/shard_map/ppermute | solution.py:164
  20.9 0.7 %shard_map.73.mine_ref = f32[1024,256]{1,0:T(8,128)S(1)} custom-call(bf16[1024,1024]{1,0:T(8,128)(2,1)S(1)} %get-tuple-element.21.tile_ref, bf16[1024,256]{1,0:T(8,128)(2,1)S(1)} %shard_map.70.ordered_ref), custom_call_target="tpu_custom_call" | custom-call | flops 10000000000 | bytes 10000000000 | tf_op jit(solution)/shard_map/pallas_call | solution.py:142
  21.7 0.9 %collective-permute-start.10 = (bf16[256,256]{1,0:T(8,128)(2,1)S(1)}, bf16[256,256]{1,0:T(8,128)(2,1)S(1)}, u32[]{:S(2)}, u32[]{:S(2)}) collective-permute-start(bf16[256,256]{1,0:T(8,128)(2,1)S(1)} %get-tuple-element.33), channel_id=1, source_target_pairs={{0,2},{1,5},{2,0},{3,7},{4,6},{5,1},{6,4},{7,3},{8,10},{9,13},{10,... | collective-permute-start | bytes 393224 | tf_op jit(solution)/shard_map/ppermute | solution.py:164
  22.7 1.2 %collective-permute-start.9 = (bf16[256,256]{1,0:T(8,128)(2,1)S(1)}, bf16[256,256]{1,0:T(8,128)(2,1)S(1)}, u32[]{:S(2)}, u32[]{:S(2)}) collective-permute-start(bf16[256,256]{1,0:T(8,128)(2,1)S(1)} %get-tuple-element.32), channel_id=1, source_target_pairs={{0,2},{1,5},{2,0},{3,7},{4,6},{5,1},{6,4},{7,3},{8,10},{9,13},{10,... | collective-permute-start | bytes 393224 | tf_op jit(solution)/shard_map/ppermute | solution.py:164
  23.8 8.1 %collective-permute-done.12.refs_2_ = bf16[256,256]{1,0:T(8,128)(2,1)S(1)} collective-permute-done((bf16[256,256]{1,0:T(8,128)(2,1)S(1)}, bf16[256,256]{1,0:T(8,128)(2,1)S(1)}, u32[]{:S(2)}, u32[]{:S(2)}) %collective-permute-start.12) | collective-permute-done | bytes 131104 | tf_op jit(solution)/shard_map/ppermute | solution.py:164
  32.1 0.9 %copy-done = bf16[512,512]{1,0:T(8,128)(2,1)S(1)} copy-done((bf16[512,512]{1,0:T(8,128)(2,1)S(1)}, bf16[512,512]{1,0:T(8,128)(2,1)}, u32[]{:S(2)}) %copy-start) | copy-done | bytes 524312
  33.2 4.7 %collective-permute-done.13.refs_2_ = bf16[256,256]{1,0:T(8,128)(2,1)S(1)} collective-permute-done((bf16[256,256]{1,0:T(8,128)(2,1)S(1)}, bf16[256,256]{1,0:T(8,128)(2,1)S(1)}, u32[]{:S(2)}, u32[]{:S(2)}) %collective-permute-start.13) | collective-permute-done | bytes 131104 | tf_op jit(solution)/shard_map/ppermute | solution.py:164
  37.9 0.9 %shard_map.77 = bf16[256,512]{1,0:T(8,128)(2,1)} custom-call(f32[512,256]{1,0:T(8,128)S(1)} %get-tuple-element.31.mine_ref.refs_0_, bf16[256,256]{1,0:T(8,128)(2,1)S(1)} %collective-permute-done.9.refs_1_, bf16[256,256]{1,0:T(8,128)(2,1)S(1)} %collective-permute-done.13.refs_2_, bf16[512,512]{1,0:T(8,128)(2,1)S(1)} %copy-done, f32[256,512]{1,0:T(8,128)S(1)} %shard_map.76.refs_4_), custom_call_target="tpu_custom_call" | custom-call | flops 1 | bytes 1 | tf_op jit(solution)/shard_map/pallas_call | solution.py:142
  (20 shorter events, 1.3 us)
Async XLA Ops:
  0.9 9.1 %collective-permute-start = (bf16[256,256]{1,0:T(8,128)(2,1)S(1)}, bf16[256,256]{1,0:T(8,128)(2,1)S(1)}, u32[]{:S(2)}, u32[]{:S(2)}) collective-permute-start(bf16[256,256]{1,0:T(8,128)(2,1)S(1)} %shard_map.65.refs_0_), channel_id=1, source_target_pairs={{0,8},{8,0},{16,24},{24,16},{1,9},{9,1},{17,25},{25,17},{2,10},{10... | collective-permute-start | bytes 393224 | tf_op jit(solution)/shard_map/ppermute | solution.py:159
  2.5 7.6 %collective-permute-start.1 = (bf16[256,256]{1,0:T(8,128)(2,1)S(1)}, bf16[256,256]{1,0:T(8,128)(2,1)S(1)}, u32[]{:S(2)}, u32[]{:S(2)}) collective-permute-start(bf16[256,256]{1,0:T(8,128)(2,1)S(1)} %shard_map.65.refs_0_), channel_id=1, source_target_pairs={{0,16},{8,24},{16,0},{24,8},{1,17},{9,25},{17,1},{25,9},{2,18},{10... | collective-permute-start | bytes 393224 | tf_op jit(solution)/shard_map/ppermute | solution.py:159
  4.0 6.9 %collective-permute-start.2 = (bf16[256,256]{1,0:T(8,128)(2,1)S(1)}, bf16[256,256]{1,0:T(8,128)(2,1)S(1)}, u32[]{:S(2)}, u32[]{:S(2)}) collective-permute-start(bf16[256,256]{1,0:T(8,128)(2,1)S(1)} %shard_map.65.refs_0_), channel_id=1, source_target_pairs={{0,24},{8,16},{16,8},{24,0},{1,25},{9,17},{17,9},{25,1},{2,26},{10... | collective-permute-start | bytes 393224 | tf_op jit(solution)/shard_map/ppermute | solution.py:159
  6.5 8.3 %collective-permute-start.4 = (bf16[256,256]{1,0:T(8,128)(2,1)S(1)}, bf16[256,256]{1,0:T(8,128)(2,1)S(1)}, u32[]{:S(2)}, u32[]{:S(2)}) collective-permute-start(bf16[256,256]{1,0:T(8,128)(2,1)S(1)} %get-tuple-element.27.refs_0_), channel_id=1, source_target_pairs={{0,8},{8,0},{16,24},{24,16},{1,9},{9,1},{17,25},{25,17},{2,10},{10... | collective-permute-start | bytes 393224 | tf_op jit(solution)/shard_map/ppermute | solution.py:159
  8.1 6.8 %collective-permute-start.5 = (bf16[256,256]{1,0:T(8,128)(2,1)S(1)}, bf16[256,256]{1,0:T(8,128)(2,1)S(1)}, u32[]{:S(2)}, u32[]{:S(2)}) collective-permute-start(bf16[256,256]{1,0:T(8,128)(2,1)S(1)} %get-tuple-element.27.refs_0_), channel_id=1, source_target_pairs={{0,16},{8,24},{16,0},{24,8},{1,17},{9,25},{17,1},{25,9},{2,18},{10... | collective-permute-start | bytes 393224 | tf_op jit(solution)/shard_map/ppermute | solution.py:159
  10.0 5.9 %collective-permute-start.6 = (bf16[256,256]{1,0:T(8,128)(2,1)S(1)}, bf16[256,256]{1,0:T(8,128)(2,1)S(1)}, u32[]{:S(2)}, u32[]{:S(2)}) collective-permute-start(bf16[256,256]{1,0:T(8,128)(2,1)S(1)} %get-tuple-element.27.refs_0_), channel_id=1, source_target_pairs={{0,24},{8,16},{16,8},{24,0},{1,25},{9,17},{17,9},{25,1},{2,26},{10... | collective-permute-start | bytes 393224 | tf_op jit(solution)/shard_map/ppermute | solution.py:159
  12.3 2.0 %collective-permute-start.3 = (bf16[1024,256]{1,0:T(8,128)(2,1)S(1)}, bf16[1024,256]{1,0:T(8,128)(2,1)S(1)}, u32[]{:S(2)}, u32[]{:S(2)}) collective-permute-start(bf16[1024,256]{1,0:T(8,128)(2,1)S(1)} %shard_map.68), channel_id=1, source_target_pairs={{0,1},{1,0},{2,3},{3,2},{4,5},{5,4},{6,7},{7,6},{8,9},{9,8},{10,11... | collective-permute-start | bytes 1572872 | tf_op jit(solution)/shard_map/ppermute | solution.py:159
  14.4 6.4 %collective-permute-start.7 = (bf16[256,256]{1,0:T(8,128)(2,1)S(1)}, bf16[256,256]{1,0:T(8,128)(2,1)S(1)}, u32[]{:S(2)}, u32[]{:S(2)}) collective-permute-start(bf16[256,256]{1,0:T(8,128)(2,1)S(1)} %get-tuple-element.28), channel_id=1, source_target_pairs={{0,2},{1,5},{2,0},{3,7},{4,6},{5,1},{6,4},{7,3},{8,10},{9,13},{10,... | collective-permute-start | bytes 393224 | tf_op jit(solution)/shard_map/ppermute | solution.py:164
  17.3 4.3 %collective-permute-start.8 = (bf16[1024,256]{1,0:T(8,128)(2,1)S(1)}, bf16[1024,256]{1,0:T(8,128)(2,1)S(1)}, u32[]{:S(2)}, u32[]{:S(2)}) collective-permute-start(bf16[1024,256]{1,0:T(8,128)(2,1)S(1)} %shard_map.71), channel_id=1, source_target_pairs={{0,1},{1,0},{2,3},{3,2},{4,5},{5,4},{6,7},{7,6},{8,9},{9,8},{10,11... | collective-permute-start | bytes 1572872 | tf_op jit(solution)/shard_map/ppermute | solution.py:159
  17.4 6.4 %collective-permute-start.11 = (bf16[256,256]{1,0:T(8,128)(2,1)S(1)}, bf16[256,256]{1,0:T(8,128)(2,1)S(1)}, u32[]{:S(2)}, u32[]{:S(2)}) collective-permute-start(bf16[256,256]{1,0:T(8,128)(2,1)S(1)} %get-tuple-element.34), channel_id=1, source_target_pairs={{0,2},{1,5},{2,0},{3,7},{4,6},{5,1},{6,4},{7,3},{8,10},{9,13},{10,... | collective-permute-start | bytes 393224 | tf_op jit(solution)/shard_map/ppermute | solution.py:164
  20.8 11.1 %collective-permute-start.12 = (bf16[256,256]{1,0:T(8,128)(2,1)S(1)}, bf16[256,256]{1,0:T(8,128)(2,1)S(1)}, u32[]{:S(2)}, u32[]{:S(2)}) collective-permute-start(bf16[256,256]{1,0:T(8,128)(2,1)S(1)} %shard_map.72), channel_id=1, source_target_pairs={{0,4},{1,3},{2,6},{3,1},{4,0},{5,7},{6,2},{7,5},{8,12},{9,11},{10,... | collective-permute-start | bytes 393224 | tf_op jit(solution)/shard_map/ppermute | solution.py:164
  21.7 10.2 %collective-permute-start.10 = (bf16[256,256]{1,0:T(8,128)(2,1)S(1)}, bf16[256,256]{1,0:T(8,128)(2,1)S(1)}, u32[]{:S(2)}, u32[]{:S(2)}) collective-permute-start(bf16[256,256]{1,0:T(8,128)(2,1)S(1)} %get-tuple-element.33), channel_id=1, source_target_pairs={{0,2},{1,5},{2,0},{3,7},{4,6},{5,1},{6,4},{7,3},{8,10},{9,13},{10,... | collective-permute-start | bytes 393224 | tf_op jit(solution)/shard_map/ppermute | solution.py:164
  22.7 10.5 %collective-permute-start.9 = (bf16[256,256]{1,0:T(8,128)(2,1)S(1)}, bf16[256,256]{1,0:T(8,128)(2,1)S(1)}, u32[]{:S(2)}, u32[]{:S(2)}) collective-permute-start(bf16[256,256]{1,0:T(8,128)(2,1)S(1)} %get-tuple-element.32), channel_id=1, source_target_pairs={{0,2},{1,5},{2,0},{3,7},{4,6},{5,1},{6,4},{7,3},{8,10},{9,13},{10,... | collective-permute-start | bytes 393224 | tf_op jit(solution)/shard_map/ppermute | solution.py:164
  32.0 1.0 %copy-start = (bf16[512,512]{1,0:T(8,128)(2,1)S(1)}, bf16[512,512]{1,0:T(8,128)(2,1)}, u32[]{:S(2)}) copy-start(bf16[512,512]{1,0:T(8,128)(2,1)} %refs_3_.3) | copy-start | bytes 1572868
  32.0 5.9 %collective-permute-start.13 = (bf16[256,256]{1,0:T(8,128)(2,1)S(1)}, bf16[256,256]{1,0:T(8,128)(2,1)S(1)}, u32[]{:S(2)}, u32[]{:S(2)}) collective-permute-start(bf16[256,256]{1,0:T(8,128)(2,1)S(1)} %shard_map.75), channel_id=1, source_target_pairs={{0,4},{1,3},{2,6},{3,1},{4,0},{5,7},{6,2},{7,5},{8,12},{9,11},{10,... | collective-permute-start | bytes 393224 | tf_op jit(solution)/shard_map/ppermute | solution.py:164
